TPU v7x, 32 devices: a whole 2x2x4 slice. The times are simulated.
32 devices in a mesh: member: 2 (over x), lat: 8 (over z, y), lon: 2 (over core).
Axes of the slice: x: 2, y: 2, z: 4, core: 2. Of those that a mesh axis runs over, the one named last changes fastest.
Arguments:
- tokens: bfloat16 [128, 192, 1024], P(('member', 'lat'), 'lon'), parts along dimension 0, may hold values from -6 to 6
- ln_gain: float32 [1024], replicated, may hold values from 0.5 to 1.5
- w_query: bfloat16 [1024, 1024], replicated, may hold values from -3 to 3
- w_keyval: bfloat16 [1024, 2048], replicated, may hold values from -3 to 3
- w_out: bfloat16 [1024, 1024], replicated, may hold values from -0.1875 to 0.1875
- w_dec: bfloat16 [1024, 512], replicated, may hold values from -0.1875 to 0.1875
- nudge: float32 [32], replicated, may hold values from 0.2 to 1
- state: float32 [32, 512, 768], P(None, ('member', 'lat'), 'lon'), parts along dimension 1, may hold values from -6 to 6
Outputs:
- advanced: float32 [32, 512, 768], P(None, ('member', 'lat', 'lon')), parts along dimension 1
There are 2 independent parts, one for each index of `member`. A program takes and returns all parts, laid end to end along the dimension named above; an argument that names none is the same for every part. Nothing has to cross between parts.
All inputs are finite; a program needn't handle non-finite values.
Results may differ from a plain program's by a relative error of at most 0.003.
Values may be sent and summed in bfloat16 or wider, within the bound.
A program may use at most 128 MiB of HBM per device.

v0:
```python
import math

import jax
import jax.numpy as jnp
from jax import lax
from jax.sharding import PartitionSpec as P

HEADS = 16
WIN = 8
PATCH = 4
VARS = 4
LEV = 8
LON_PIX = 768
KEEP = 256


time_step = 0.1
diffusion = 0.5
epsilon = 1e-05


def padded_2(x, sides, width, wrap):
    for axis, dim in sides:
        size, length = (lax.axis_size(axis), x.shape[dim])
        up = [(i, (i + 1) % size) for i in range(size if wrap else size - 1)]
        down = [(j, i) for i, j in up]
        last = lax.slice_in_dim(x, length - width, length, axis=dim)
        first = lax.slice_in_dim(x, 0, width, axis=dim)
        before = lax.ppermute(last, axis, up)
        after = lax.ppermute(first, axis, down)
        x = jnp.concatenate([before, x, after], axis=dim)
    return x


def layer_norm(inputs, gain_vector):
    centred = inputs - jnp.mean(inputs, axis=-1, keepdims=True)
    variance = jnp.mean(centred * centred, axis=-1, keepdims=True)
    return (centred * lax.rsqrt(variance + epsilon) * gain_vector).astype(jnp.bfloat16)


def to_windows(tensor, row_blocks, col_blocks):
    features = tensor.shape[-1]
    shaped = tensor.reshape(row_blocks, WIN, col_blocks, WIN, features)
    return shaped.transpose(0, 2, 1, 3, 4).reshape(row_blocks * col_blocks, WIN * WIN, features)


def from_windows(tensor, row_blocks, col_blocks):
    features = tensor.shape[-1]
    shaped = tensor.reshape(row_blocks, col_blocks, WIN, WIN, features)
    return shaped.transpose(0, 2, 1, 3, 4).reshape(row_blocks * WIN, col_blocks * WIN, features)


def window_attention(queries, keyval_win, key_valid):
    windows_count, window_cells, model_width = queries.shape
    head_size = model_width // HEADS
    query_heads = queries.reshape(windows_count, window_cells, HEADS, head_size)
    key_heads = keyval_win[..., :model_width].reshape(windows_count, window_cells, HEADS, head_size)
    value_heads = keyval_win[..., model_width:].reshape(
        windows_count, window_cells, HEADS, head_size
    )
    scores = jnp.einsum(
        "wqhd,wkhd->whqk", query_heads, key_heads, preferred_element_type=jnp.float32
    ) / math.sqrt(head_size)
    scores = jnp.where(key_valid[:, None, None, :], scores, -1e30)
    peak_score = jnp.max(scores, axis=-1, keepdims=True)
    weights = jnp.exp(scores - peak_score)
    weights = (weights / jnp.sum(weights, axis=-1, keepdims=True)).astype(jnp.bfloat16)
    mixed_out = jnp.einsum(
        "whqk,wkhd->wqhd", weights, value_heads, preferred_element_type=jnp.float32
    )
    return mixed_out.astype(jnp.bfloat16).reshape(windows_count, window_cells, model_width)


def zonal_basis(length, kept_waves):
    columns = jnp.arange(length, dtype=jnp.int32)
    wave_index = jnp.arange(kept_waves, dtype=jnp.int32)
    winding = columns[:, None] * wave_index[None, :] % length
    phases = winding.astype(jnp.float32) * (2.0 * math.pi / length)
    basis_table = jnp.concatenate([jnp.cos(phases), jnp.sin(phases)], axis=1)
    factor = jnp.where(wave_index == 0, 1.0, 2.0).astype(jnp.float32) / length
    return (basis_table, jnp.concatenate([factor, factor]))


def tendency(padded):
    centre = padded[:, 1:-1, 1:-1]
    east_cell = padded[:, 1:-1, 2:]
    west_cell = padded[:, 1:-1, :-2]
    north_cell = padded[:, 2:, 1:-1]
    south_cell = padded[:, :-2, 1:-1]
    field_shape = (VARS, LEV) + centre.shape[1:]
    wind_u = centre[:LEV][None]
    wind_v = centre[LEV : 2 * LEV][None]
    advection = wind_u * (east_cell - west_cell).reshape(field_shape) * 0.5
    advection = advection + wind_v * (north_cell - south_cell).reshape(field_shape) * 0.5
    spread_term = diffusion * (east_cell + west_cell + north_cell + south_cell - 4.0 * centre)
    return spread_term - advection.reshape(centre.shape)


def row_mask(padded, first_row, total_rows, depth):
    row_ids = first_row - depth + jnp.arange(padded.shape[1], dtype=jnp.int32)
    inside = ((row_ids >= 0) & (row_ids < total_rows)).astype(jnp.float32)
    return padded * inside[None, :, None]


def wrap_columns(padded, depth):
    return jnp.concatenate([padded[..., -depth:], padded, padded[..., :depth]], axis=2)


def advance(nudged, extend_one, first_row, total_rows):
    first_section = nudged + time_step * tendency(
        row_mask(extend_one(nudged), first_row, total_rows, 1)
    )
    second = tendency(row_mask(extend_one(first_section), first_row, total_rows, 1))
    return 0.5 * (nudged + first_section + time_step * second)


def decoded_coeffs(decoded_flat, patch_basis):
    channels_all = decoded_flat.shape[0] // (PATCH * PATCH)
    shaped = decoded_flat.reshape(
        channels_all, PATCH, PATCH, decoded_flat.shape[1], decoded_flat.shape[2]
    )
    result = jnp.einsum(
        "kabrc,bcw->kraw",
        shaped,
        patch_basis,
        precision=lax.Precision.HIGHEST,
        preferred_element_type=jnp.float32,
    )
    return result.reshape(-1, patch_basis.shape[2])


def body(tokens, ln_gain, w_query, w_keyval, w_out, w_dec, nudge, state):
    tok_rows, tok_cols, model_width = tokens.shape
    half_win = WIN // 2
    inputs = tokens.astype(jnp.float32)
    normed = layer_norm(inputs, ln_gain)
    flat_rows = normed.reshape(tok_rows * tok_cols, model_width)
    queries = jnp.dot(flat_rows, w_query, preferred_element_type=jnp.float32).astype(jnp.bfloat16)
    queries = queries.reshape(tok_rows, tok_cols, model_width)
    rim_tokens = padded_2(normed, (("lat", 0), ("lon", 1)), half_win, True)
    keyval = jnp.dot(
        rim_tokens.reshape(-1, model_width), w_keyval, preferred_element_type=jnp.float32
    ).astype(jnp.bfloat16)
    keyval = keyval.reshape(tok_rows + WIN, tok_cols + WIN, 2 * model_width)
    row_blocks = tok_rows // WIN + 1
    col_blocks = tok_cols // WIN + 1
    padded_queries = jnp.pad(queries, ((half_win, half_win), (half_win, half_win), (0, 0)))
    global_row = (
        lax.axis_index("lat") * tok_rows - half_win + jnp.arange(tok_rows + WIN, dtype=jnp.int32)
    )
    inside = ((global_row >= 0) & (global_row < tok_rows * lax.axis_size("lat"))).astype(jnp.int32)
    inside_grid = jnp.broadcast_to(inside[:, None, None], (tok_rows + WIN, tok_cols + WIN, 1))
    key_valid = to_windows(inside_grid, row_blocks, col_blocks)[..., 0] > 0
    attended = window_attention(
        to_windows(padded_queries, row_blocks, col_blocks),
        to_windows(keyval, row_blocks, col_blocks),
        key_valid,
    )
    attended = from_windows(attended, row_blocks, col_blocks)
    attended = attended[half_win : half_win + tok_rows, half_win : half_win + tok_cols]
    update = jnp.dot(attended.reshape(-1, model_width), w_out, preferred_element_type=jnp.float32)
    layer_out = (inputs.reshape(-1, model_width) + update).astype(jnp.bfloat16)
    decoded = jnp.einsum(
        "dm,rcd->mrc",
        w_dec,
        layer_out.reshape(tok_rows, tok_cols, model_width),
        preferred_element_type=jnp.float32,
    )
    basis_table, factor = zonal_basis(LON_PIX, KEEP)
    total_cols = LON_PIX // PATCH
    patch_basis = basis_table.reshape(total_cols, PATCH, 2 * KEEP).transpose(1, 0, 2)
    nudge_scale = nudge[:, None, None]
    band_dec, band_state = (
        lax.all_to_all(decoded, "lon", split_axis=1, concat_axis=2, tiled=True),
        lax.all_to_all(state, "lon", split_axis=1, concat_axis=2, tiled=True),
    )
    band_rows = band_state.shape[1]
    state_coeffs = jnp.dot(
        band_state.reshape(-1, band_state.shape[2]),
        basis_table,
        precision=lax.Precision.HIGHEST,
        preferred_element_type=jnp.float32,
    )
    coefficients = decoded_coeffs(band_dec, patch_basis) - state_coeffs
    filtered = jnp.dot(
        coefficients * factor,
        basis_table.T,
        precision=lax.Precision.HIGHEST,
        preferred_element_type=jnp.float32,
    )
    nudged = band_state + nudge_scale * filtered.reshape(band_state.shape)

    def extend_one(field):
        rows_added = padded_2(field.astype(jnp.bfloat16), ((("lat", "lon"), 1),), 1, False).astype(
            field.dtype
        )
        return wrap_columns(rows_added, 1)

    return advance(
        nudged,
        extend_one,
        lax.axis_index(("lat", "lon")) * band_rows,
        band_rows * lax.axis_size(("lat", "lon")),
    )


def solution(mesh):
    in_specs = (
        P(("member", "lat"), "lon", None),
        P(),
        P(),
        P(),
        P(),
        P(),
        P(),
        P(None, ("member", "lat"), "lon"),
    )
    out_specs = P(None, ("member", "lat", "lon"), None)
    return jax.shard_map(body, mesh=mesh, in_specs=in_specs, out_specs=out_specs, check_vma=False)
```

profile of v0, /device:TPU:21, one launch (start us, length us, event | category | flops | bytes accessed | tf_op | source)
XLA Modules:
  0.0 216.8 jit_solution(11118138513977932381)
XLA Ops:
  7.1 2.1 copy.49
  9.1 6.0 %all-to-all-start = ((f32[32,32,384]{2,0,1:T(8,128)}), f32[32,32,384]{2,0,1:T(8,128)}, u32[]{:S(2)}, u32[]{:S(2)}) async-start(f32[32,32,384]{2,0,1:T(8,128)} %copy.49), calls=%async_computation | async-start | bytes 3145728 | tf_op jit(solution)/shard_map/all_to_all | solution.py:175
  15.2 4.2 %fusion.43 = (f32[768,256]{1,0:T(8,128)S(1)}, f32[768,256]{1,0:T(8,128)}) fusion(), kind=kLoop, calls=%fused_computation.70 | loop fusion | flops 1769472 | bytes 1572864 | tf_op jit(solution)/shard_map/sin | solution.py:79
  19.3 4.6 %fusion.48 = (f32[192,4,256]{2,0,1:T(8,128)}, f32[192,4,256]{2,0,1:T(8,128)}) fusion(s32[192,4]{0,1:T(4,128)S(1)} %multiply_add_fusion.1), kind=kLoop, calls=%fused_computation.76 | loop fusion | flops 1769472 | bytes 1575936 | tf_op jit(solution)/shard_map/cos | solution.py:79
  23.9 4.5 %convolution_convert_fusion.2 = bf16[768,1024]{1,0:T(8,128)(2,1)} fusion(bf16[768,1024]{1,0:T(8,128)(2,1)} %bitcast.98, bf16[1024,1024]{1,0:T(8,128)(2,1)S(1)} %copy-done), kind=kOutput, calls=%fused_computation.25 | convolution fusion | flops 1611399168 | bytes 5242880 | tf_op jit(solution)/shard_map/dot_general | solution.py:138
  28.4 12.7 %collective-permute-done = bf16[4,96,1024]{2,1,0:T(8,128)(2,1)} collective-permute-done((bf16[4,96,1024]{2,1,0:T(8,128)(2,1)}, bf16[4,96,1024]{2,1,0:T(8,128)(2,1)}, u32[]{:S(2)}, u32[]{:S(2)}) %collective-permute-start) | collective-permute-done | bytes 786464 | tf_op jit(solution)/shard_map/ppermute | solution.py:29
  44.6 2.1 copy.53
  46.7 9.6 %reshape_reshape.10 = bf16[26,64,16,64]{3,2,1,0:T(8,128)(2,1)} reshape(bf16[2,13,8,8,1024]{4,3,2,1,0:T(8,128)(2,1)} %copy.53) | data formatting | bytes 6815744 | tf_op jit(solution)/shard_map/reshape;reshape | solution.py:56
  56.5 2.6 %copy.85 = f32[32,2,16,384]{3,1,2,0:T(2,128)S(1)} copy(f32[32,2,16,384]{3,0,2,1:T(8,128)} %bitcast) | data formatting | bytes 3145728 | tf_op jit(solution)/shard_map/all_to_all | solution.py:175
  61.5 3.5 %all_to_all.27 = f32[32,16,768]{2,1,0:T(8,128)} reshape(f32[32,16,2,384]{3,2,1,0:T(2,128)} %bitcast.100) | data formatting | bytes 3145728 | tf_op jit(solution)/shard_map/all_to_all | solution.py:175
  65.0 3.2 %pad_maximum_fusion = bf16[16,104,1024]{2,1,0:T(8,128)(2,1)S(1)} fusion(bf16[16,4,1024]{2,1,0:T(4,128)(2,1)S(1)} %collective-permute-done.3, bf16[4,96,1024]{2,1,0:T(8,128)(2,1)} %collective-permute-done.1, bf16[8,96,1024]{2,1,0:T(8,128)(2,1)S(1)} %copy-done.4, bf16[4,96,1024]{2,1,0:T(8,128)(2,1)} %collective-permute-done, ...), kind=kLoop, calls=%fused_computation.15 | loop fusion | flops 17039360 | bytes 6815744 | tf_op jit(solution)/shard_map/concatenate | solution.py:31
  68.3 9.8 %convolution_convert_fusion = bf16[1664,2048]{1,0:T(8,128)(2,1)} fusion(bf16[1664,1024]{1,0:T(8,128)(2,1)S(1)} %bitcast.110, bf16[1024,2048]{1,0:T(8,128)(2,1)S(1)} %copy-done.14), kind=kOutput, calls=%fused_computation.5 | convolution fusion | flops 6982729728 | bytes 14417920 | tf_op jit(solution)/shard_map/dot_general | solution.py:141
  78.0 3.8 %copy.51 = bf16[2,8,13,8,2048]{4,3,1,2,0:T(8,128)(2,1)S(1)} copy(bf16[2,8,13,8,2048]{4,3,2,1,0:T(8,128)(2,1)} %bitcast.106) | data formatting | bytes 13631488 | tf_op jit(solution)/shard_map/reshape;reshape | solution.py:43
  81.8 3.6 %fusion.61 = (bf16[26,64,1024]{2,1,0:T(8,128)(2,1)}, bf16[26,64,1024]{2,1,0:T(8,128)(2,1)}) fusion(bf16[26,64,2048]{2,1,0:T(8,128)(2,1)S(1)} %bitcast.97), kind=kLoop, calls=%fused_computation.99 | loop fusion | bytes 13631488 | tf_op jit(solution)/shard_map/slice | solution.py:57
  85.4 9.6 %reshape.135 = bf16[26,64,16,64]{3,2,1,0:T(8,128)(2,1)} reshape(bf16[26,64,1024]{2,1,0:T(8,128)(2,1)} %get-tuple-element.9) | data formatting | bytes 6815744 | tf_op jit(solution)/shard_map/reshape | solution.py:57
  95.0 7.3 %copy.52 = bf16[26,64,1024]{1,2,0:T(8,128)(2,1)} copy(bf16[26,64,1024]{2,1,0:T(8,128)(2,1)} %get-tuple-element.10) | data formatting | bytes 6815744 | tf_op jit(solution)/shard_map/slice | solution.py:58
  102.4 13.4 %fusion.70 = (f32[26,16,64]{2,1,0:T(8,128)S(1)}, f32[26,16,64,64]{2,3,1,0:T(8,128)}) fusion(pred[26,64]{1,0:T(8,128)(4,1)S(1)} %gt.13, bf16[26,64,16,64]{3,2,1,0:T(8,128)(2,1)} %reshape.135, bf16[26,64,16,64]{3,2,1,0:T(8,128)(2,1)} %reshape_reshape.10), kind=kOutput, calls=%fused_computation.108 | convolution fusion | flops 224919616 | bytes 13739648 | tf_op jit(solution)/shard_map/sub | solution.py:66
  115.7 11.5 %fusion.9 = bf16[26,64,16,64]{1,3,2,0:T(8,128)(2,1)} fusion(bf16[26,64,16,64]{1,3,2,0:T(8,128)(2,1)} %bitcast.105, f32[26,16,64,64]{2,3,1,0:T(8,128)} %get-tuple-element.32, f32[26,16,64]{2,1,0:T(8,128)S(1)} %get-tuple-element.31), kind=kOutput, calls=%fused_computation.14 | convolution fusion | flops 223215616 | bytes 13737984 | tf_op jit(solution)/shard_map/whqk,wkhd->wqhd/dot_general | solution.py:68
  127.2 10.5 %copy.57 = bf16[26,64,16,64]{3,2,1,0:T(8,128)(2,1)} copy(bf16[26,64,16,64]{1,3,2,0:T(8,128)(2,1)} %fusion.9) | data formatting | bytes 6815744 | tf_op jit(solution)/shard_map/convert_element_type | solution.py:71
  137.7 9.9 %reshape_reshape.11 = bf16[2,13,8,8,1024]{4,3,2,1,0:T(8,128)(2,1)} reshape(bf16[26,64,16,64]{3,2,1,0:T(8,128)(2,1)} %copy.57) | data formatting | bytes 6815744 | tf_op jit(solution)/shard_map/reshape;reshape | solution.py:49
  147.6 2.5 %copy.58 = bf16[2,8,13,8,1024]{4,3,2,1,0:T(8,128)(2,1)S(1)} copy(bf16[2,8,13,8,1024]{4,3,1,2,0:T(8,128)(2,1)} %bitcast.101) | data formatting | bytes 6815744 | tf_op jit(solution)/shard_map/transpose | solution.py:50
  154.3 5.9 %all_to_all.33 = f32[512,8,96]{0,2,1:T(8,128)} all-to-all(f32[512,8,96]{0,2,1:T(8,128)S(1)} %convolution_bitcast_fusion), channel_id=1, replica_groups=mesh['member'=2,'lat'=8,'lon'=2] {'lon'}, dimensions={1} | all-to-all | bytes 3145728 | tf_op jit(solution)/shard_map/all_to_all | solution.py:174
  160.2 3.1 %copy.59 = f32[512,2,4,96]{3,1,2,0:T(2,128)S(1)} copy(f32[512,2,4,96]{0,3,2,1:T(8,128)} %bitcast.107) | data formatting | bytes 3145728 | tf_op jit(solution)/shard_map/all_to_all | solution.py:174
  163.3 2.8 %reshape.139 = f32[32,4,4,4,192]{4,3,2,1,0:T(4,128)} reshape(f32[512,4,2,96]{3,2,1,0:T(2,128)S(1)} %bitcast.103) | data formatting | bytes 3145728 | tf_op jit(solution)/shard_map/reshape | solution.py:119
  166.1 5.8 %fusion.30 = f32[32,4,4,512]{3,0,1,2:T(8,128)S(1)} fusion(f32[32,4,4,4,192]{4,3,2,1,0:T(4,128)} %reshape.139, f32[192,4,256]{2,0,1:T(8,128)} %get-tuple-element.30, f32[192,4,256]{2,0,1:T(8,128)} %get-tuple-element.29), kind=kOutput, calls=%fused_computation.53 | convolution fusion | flops 2416312320 | bytes 4194304 | tf_op jit(solution)/shard_map/kabrc,bcw->kraw/dot_general | solution.py:122
  175.5 6.5 %fusion.34 = f32[512,512]{0,1:T(8,128)S(1)} fusion(f32[512,512]{0,1:T(8,128)S(1)} %copy.62, f32[512,768]{1,0:T(8,128)} %bitcast.108, f32[768,256]{1,0:T(8,128)S(1)} %get-tuple-element.33, f32[768,256]{1,0:T(8,128)S(1)} %copy-done.8, f32[512]{0:T(512)S(1)} %pad_maximum_fusion.7), kind=kOutput, calls=%fused_computation.56 | convolution fusion | flops 2416836608 | bytes 5244928 | tf_op jit(solution)/shard_map/dot_general | solution.py:178
  182.1 5.4 %fusion.35 = f32[512,768]{1,0:T(8,128)S(1)} fusion(f32[512,512]{0,1:T(8,128)S(1)} %fusion.34, f32[768,256]{1,0:T(8,128)S(1)} %get-tuple-element.33, f32[768,256]{1,0:T(8,128)S(1)} %copy-done.8), kind=kOutput, calls=%fused_computation.57 | convolution fusion | flops 2416312320 | bytes 4194304 | tf_op jit(solution)/shard_map/dot_general | solution.py:185
  187.9 4.3 %collective-permute-start.4 = (bf16[32,1,768]{2,1,0:T(2,128)(2,1)S(1)}, bf16[32,1,768]{2,1,0:T(2,128)(2,1)S(1)}, u32[]{:S(2)}, u32[]{:S(2)}) collective-permute-start(bf16[32,1,768]{2,1,0:T(2,128)(2,1)S(1)} %get-tuple-element.27), channel_id=1, source_target_pairs={{0,1},{1,2},{2,3},{3,4},{4,5},{5,6},{6,7},{7,8},{8,9},{9,10},{10,1... | collective-permute-start | bytes 147464 | tf_op jit(solution)/shard_map/ppermute | solution.py:29
  194.2 4.9 %collective-permute-done.5 = bf16[32,1,768]{2,1,0:T(2,128)(2,1)S(1)} collective-permute-done((bf16[32,1,768]{2,1,0:T(2,128)(2,1)S(1)}, bf16[32,1,768]{2,1,0:T(2,128)(2,1)S(1)}, u32[]{:S(2)}, u32[]{:S(2)}) %collective-permute-start.5) | collective-permute-done | bytes 49184 | tf_op jit(solution)/shard_map/ppermute | solution.py:30
  204.9 2.4 %collective-permute-start.7 = (bf16[32,1,768]{2,1,0:T(2,128)(2,1)S(1)}, bf16[32,1,768]{2,1,0:T(2,128)(2,1)S(1)}, u32[]{:S(2)}, u32[]{:S(2)}) collective-permute-start(bf16[32,1,768]{2,1,0:T(2,128)(2,1)S(1)} %get-tuple-element.26), channel_id=1, source_target_pairs={{1,0},{2,1},{3,2},{4,3},{5,4},{6,5},{7,6},{8,7},{9,8},{10,9},{11,1... | collective-permute-start | bytes 147464 | tf_op jit(solution)/shard_map/ppermute | solution.py:30
  207.3 4.4 %collective-permute-done.7 = bf16[32,1,768]{2,1,0:T(2,128)(2,1)S(1)} collective-permute-done((bf16[32,1,768]{2,1,0:T(2,128)(2,1)S(1)}, bf16[32,1,768]{2,1,0:T(2,128)(2,1)S(1)}, u32[]{:S(2)}, u32[]{:S(2)}) %collective-permute-start.7) | collective-permute-done | bytes 49184 | tf_op jit(solution)/shard_map/ppermute | solution.py:30
  213.6 3.0 %fusion.18 = f32[32,16,768]{2,1,0:T(8,128)} fusion(f32[32,18,770]{2,1,0:T(8,128)S(1)} %maximum_multiply_fusion.1, f32[32,16,768]{2,1,0:T(8,128)S(1)} %get-tuple-element.8, f32[32,16,768]{2,1,0:T(8,128)S(1)} %get-tuple-element.6, f32[8,16,768]{2,1,0:T(8,128)S(1)} %get-tuple-element.14, f32[8,16,768]{2,1,0:T(8,128)S(1)} %get-tuple-element.13), kind=kLoop, calls=%fused_computation.32 | loop fusion | flops 6684672 | bytes 13369344 | tf_op jit(solution)/shard_map/mul | solution.py:114
  (80 shorter events, 30.8 us)
Async XLA Ops:
  0.0 23.9 %copy-start = (bf16[1024,1024]{1,0:T(8,128)(2,1)S(1)}, bf16[1024,1024]{1,0:T(8,128)(2,1)}, u32[]{:S(2)}) copy-start(bf16[1024,1024]{1,0:T(8,128)(2,1)} %param.10) | copy-start | bytes 6291460
  0.0 2.0 copy-start.5
  0.0 2.6 %copy-start.12 = (f32[1024]{0:T(1024)S(1)}, f32[1024]{0:T(1024)}, u32[]{:S(2)}) copy-start(f32[1024]{0:T(1024)} %param.9) | copy-start | bytes 12292
  3.2 1.2 copy-start.2
  4.3 2.7 %copy-start.11 = (f32[32,32,384]{2,1,0:T(8,128)S(1)}, f32[32,32,384]{2,1,0:T(8,128)}, u32[]{:S(2)}) copy-start(f32[32,32,384]{2,1,0:T(8,128)} %param.15) | copy-start | bytes 4718596
  5.6 35.6 %collective-permute-start = (bf16[4,96,1024]{2,1,0:T(8,128)(2,1)}, bf16[4,96,1024]{2,1,0:T(8,128)(2,1)}, u32[]{:S(2)}, u32[]{:S(2)}) collective-permute-start(bf16[4,96,1024]{2,1,0:T(8,128)(2,1)} %get-tuple-element.23), channel_id=1, source_target_pairs={{0,2},{2,4},{4,6},{6,8},{8,10},{10,12},{12,14},{14,0},{1,3},{3,5},... | collective-permute-start | bytes 2359304 | tf_op jit(solution)/shard_map/ppermute | solution.py:29
  6.8 34.4 %collective-permute-start.1 = (bf16[4,96,1024]{2,1,0:T(8,128)(2,1)}, bf16[4,96,1024]{2,1,0:T(8,128)(2,1)}, u32[]{:S(2)}, u32[]{:S(2)}) collective-permute-start(bf16[4,96,1024]{2,1,0:T(8,128)(2,1)} %get-tuple-element.24), channel_id=1, source_target_pairs={{2,0},{4,2},{6,4},{8,6},{10,8},{12,10},{14,12},{0,14},{3,1},{5,3},... | collective-permute-start | bytes 2359304 | tf_op jit(solution)/shard_map/ppermute | solution.py:30
  9.1 47.4 %all-to-all-start = ((f32[32,32,384]{2,0,1:T(8,128)}), f32[32,32,384]{2,0,1:T(8,128)}, u32[]{:S(2)}, u32[]{:S(2)}) async-start(f32[32,32,384]{2,0,1:T(8,128)} %copy.49), calls=%async_computation | async-start | bytes 3145728 | tf_op jit(solution)/shard_map/all_to_all | solution.py:175
  23.9 17.3 %copy-start.3 = (bf16[8,96,1024]{2,1,0:T(8,128)(2,1)S(1)}, bf16[8,96,1024]{2,1,0:T(8,128)(2,1)}, u32[]{:S(2)}) copy-start(bf16[8,96,1024]{2,1,0:T(8,128)(2,1)} %copy-done.2) | copy-start | bytes 4718596
  28.4 15.5 %copy-start.10 = (bf16[768,1024]{1,0:T(8,128)(2,1)S(1)}, bf16[768,1024]{1,0:T(8,128)(2,1)}, u32[]{:S(2)}) copy-start(bf16[768,1024]{1,0:T(8,128)(2,1)} %convolution_convert_fusion.2) | copy-start | bytes 4718596
  42.2 22.8 %collective-permute-start.2 = (bf16[16,4,1024]{2,1,0:T(4,128)(2,1)S(1)}, bf16[16,4,1024]{2,1,0:T(4,128)(2,1)S(1)}, u32[]{:S(2)}, u32[]{:S(2)}) collective-permute-start(bf16[16,4,1024]{2,1,0:T(4,128)(2,1)S(1)} %get-tuple-element.11), channel_id=1, source_target_pairs={{0,1},{1,0},{2,3},{3,2},{4,5},{5,4},{6,7},{7,6},{8,9},{9,8},{10,11... | collective-permute-start | bytes 393224 | tf_op jit(solution)/shard_map/ppermute | solution.py:29
  43.8 21.2 %collective-permute-start.3 = (bf16[16,4,1024]{2,1,0:T(4,128)(2,1)S(1)}, bf16[16,4,1024]{2,1,0:T(4,128)(2,1)S(1)}, u32[]{:S(2)}, u32[]{:S(2)}) collective-permute-start(bf16[16,4,1024]{2,1,0:T(4,128)(2,1)S(1)} %get-tuple-element.12), channel_id=1, source_target_pairs={{1,0},{0,1},{3,2},{2,3},{5,4},{4,5},{7,6},{6,7},{9,8},{8,9},{11,10... | collective-permute-start | bytes 393224 | tf_op jit(solution)/shard_map/ppermute | solution.py:30
  59.1 1.1 copy-start.7
  61.5 3.5 %copy-start.4 = (bf16[8,96,1024]{2,1,0:T(8,128)(2,1)S(1)}, bf16[8,96,1024]{2,1,0:T(8,128)(2,1)}, u32[]{:S(2)}) copy-start(bf16[8,96,1024]{2,1,0:T(8,128)(2,1)} %copy-done.2) | copy-start | bytes 4718596
  65.0 3.2 %copy-start.14 = (bf16[1024,2048]{1,0:T(8,128)(2,1)S(1)}, bf16[1024,2048]{1,0:T(8,128)(2,1)}, u32[]{:S(2)}) copy-start(bf16[1024,2048]{1,0:T(8,128)(2,1)} %param.11) | copy-start | bytes 12582916
  147.6 2.9 %copy-start.15 = (bf16[1024,1024]{1,0:T(8,128)(2,1)S(1)}, bf16[1024,1024]{1,0:T(8,128)(2,1)}, u32[]{:S(2)}) copy-start(bf16[1024,1024]{1,0:T(8,128)(2,1)} %param.12) | copy-start | bytes 6291460
  150.0 1.4 copy-start.6
  151.5 1.8 copy-start.16
  172.6 2.9 %copy-start.8 = (f32[768,256]{1,0:T(8,128)S(1)}, f32[768,256]{1,0:T(8,128)}, u32[]{:S(2)}) copy-start(f32[768,256]{1,0:T(8,128)} %get-tuple-element.34) | copy-start | bytes 2359300
  182.1 5.4 %copy-start.9 = (f32[32,16,768]{2,1,0:T(8,128)S(1)}, f32[32,16,768]{2,1,0:T(8,128)}, u32[]{:S(2)}) copy-start(f32[32,16,768]{2,1,0:T(8,128)} %all_to_all.27) | copy-start | bytes 4718596
  182.1 5.4 %copy-start.13 = (f32[32]{0:T(128)S(1)}, f32[32]{0:T(128)}, u32[]{:S(2)}) copy-start(f32[32]{0:T(128)} %param.14) | copy-start | bytes 388
  187.9 6.3 %collective-permute-start.4 = (bf16[32,1,768]{2,1,0:T(2,128)(2,1)S(1)}, bf16[32,1,768]{2,1,0:T(2,128)(2,1)S(1)}, u32[]{:S(2)}, u32[]{:S(2)}) collective-permute-start(bf16[32,1,768]{2,1,0:T(2,128)(2,1)S(1)} %get-tuple-element.27), channel_id=1, source_target_pairs={{0,1},{1,2},{2,3},{3,4},{4,5},{5,6},{6,7},{7,8},{8,9},{9,10},{10,1... | collective-permute-start | bytes 147464 | tf_op jit(solution)/shard_map/ppermute | solution.py:29
  192.2 6.8 %collective-permute-start.5 = (bf16[32,1,768]{2,1,0:T(2,128)(2,1)S(1)}, bf16[32,1,768]{2,1,0:T(2,128)(2,1)S(1)}, u32[]{:S(2)}, u32[]{:S(2)}) collective-permute-start(bf16[32,1,768]{2,1,0:T(2,128)(2,1)S(1)} %get-tuple-element.28), channel_id=1, source_target_pairs={{1,0},{2,1},{3,2},{4,3},{5,4},{6,5},{7,6},{8,7},{9,8},{10,9},{11,1... | collective-permute-start | bytes 147464 | tf_op jit(solution)/shard_map/ppermute | solution.py:30
  203.0 4.3 %collective-permute-start.6 = (bf16[32,1,768]{2,1,0:T(2,128)(2,1)S(1)}, bf16[32,1,768]{2,1,0:T(2,128)(2,1)S(1)}, u32[]{:S(2)}, u32[]{:S(2)}) collective-permute-start(bf16[32,1,768]{2,1,0:T(2,128)(2,1)S(1)} %get-tuple-element.25), channel_id=1, source_target_pairs={{0,1},{1,2},{2,3},{3,4},{4,5},{5,6},{6,7},{7,8},{8,9},{9,10},{10,1... | collective-permute-start | bytes 147464 | tf_op jit(solution)/shard_map/ppermute | solution.py:29
  204.9 6.8 %collective-permute-start.7 = (bf16[32,1,768]{2,1,0:T(2,128)(2,1)S(1)}, bf16[32,1,768]{2,1,0:T(2,128)(2,1)S(1)}, u32[]{:S(2)}, u32[]{:S(2)}) collective-permute-start(bf16[32,1,768]{2,1,0:T(2,128)(2,1)S(1)} %get-tuple-element.26), channel_id=1, source_target_pairs={{1,0},{2,1},{3,2},{4,3},{5,4},{6,5},{7,6},{8,7},{9,8},{10,9},{11,1... | collective-permute-start | bytes 147464 | tf_op jit(solution)/shard_map/ppermute | solution.py:30
  213.6 3.0 %copy-start.1 = (bf16[1024,1024]{1,0:T(8,128)(2,1)S(1)}, bf16[1024,1024]{1,0:T(8,128)(2,1)}, u32[]{:S(2)}) copy-start(bf16[1024,1024]{1,0:T(8,128)(2,1)} %param.10) | copy-start | bytes 6291460
where the time goes:
time: 221 us; the launch traced here: 217 us
  local copies, waits for them, and re-layouts  85 us (38%)
  matrix products  59.7 us (27%)
  other arithmetic  23.8 us (11%)
  waiting for transfers between devices  22 us (10%)
  starting transfers between devices  19.7 us (9%)
  blocking collectives  5.9 us (3%)
    sub x1, matrix products, window_attention(): weights = jnp.exp(scores - peak_score)  13.4 us
    ppermute x4, waiting for transfers between devices, padded_2(): before = lax.ppermute(last, axis, up)  12.7 us
    dot_general x1, matrix products, window_attention(): jnp.einsum('whqk,wkhd->wqhd', weights, value_heads, preferred_element_typ...  11.5 us
    convert_element_type x1, local copies, waits for them, and re-layouts, window_attention(): mixed_out.astype(jnp.bfloat16)  10.5 us
    another operation x1, local copies, waits for them, and re-layouts, from_windows(): shaped = tensor.reshape(row_blocks, col_blocks, WIN, WIN, features)  9.87 us
    dot_general x1, matrix products, body(): jnp.dot(rim_tokens.reshape(-1, model_width), w_keyval, preferred_element_...  9.76 us
    reshape x1, local copies, waits for them, and re-layouts, window_attention(): keyval_win[..., :model_width]  9.63 us
    another operation x1, local copies, waits for them, and re-layouts, window_attention(): query_heads = queries.reshape(windows_count, window_cells, HEADS, head_size)  9.6 us
  transfers between devices with their start and end apart: 9, of which 3 were waited for; matrix products, arithmetic and copies ran while one was open for 15% of the time, Pallas kernels for 0%

commit v1 on v0

v1 whole, which is shorter than its diff:
```python
import functools
import math

import jax
import jax.numpy as jnp
import ml_dtypes
import numpy as np
from jax import lax
from jax.experimental import pallas as pl
from jax.experimental.pallas import tpu as pltpu
from jax.sharding import PartitionSpec as P

HEADS = 16
WIN = 8
PATCH = 4
VARS = 4
LEV = 8
KEEP = 256

time_step = 0.1
diffusion = 0.5
epsilon = 1e-05
F32 = jnp.float32
BF16 = jnp.bfloat16
NT = (((1,), (1,)), ((), ()))


def full_spec(shape):
    zeros = (0,) * len(shape)
    return pl.BlockSpec(shape, lambda *_: zeros, pipeline_mode=pl.Buffered(1))


def filter_tables(length, kept):
    offset = np.arange(length)
    waves = np.arange(1, kept)
    kernel = (1.0 + 2.0 * np.cos(2.0 * np.pi * ((offset[:, None] * waves[None, :]) % length) / length).sum(1)) / length
    table = kernel[(offset[None, :] - offset[:, None]) % length].astype(np.float32)
    high = table.astype(ml_dtypes.bfloat16)
    low = (table - high.astype(np.float32)).astype(ml_dtypes.bfloat16)
    return high, low


def layer_kernel(sizes, valid_ref, gain_ref, wq_ref, wkv_ref, wo_ref, wd_ref, *rest):
    rows, cols, cw = sizes
    x_refs, (dec_ref, att, lo) = rest[:-3], rest[-3:]
    step = pl.program_id(0)
    width = wq_ref.shape[0]
    nw = cw // WIN
    cells = rows * WIN
    parts = [r[...].astype(F32).reshape(r.shape[0], nw, WIN, width) for r in x_refs]
    x = parts[0] if len(parts) == 1 else jnp.concatenate(parts, axis=0)
    x = jnp.swapaxes(x, 0, 1).reshape(nw * cells, width)
    centred = x - jnp.mean(x, axis=-1, keepdims=True)
    variance = jnp.mean(centred * centred, axis=-1, keepdims=True)
    normed = (centred * lax.rsqrt(variance + epsilon) * gain_ref[...]).astype(BF16)
    head = width // HEADS
    q = jnp.dot(normed, wq_ref[...], preferred_element_type=F32).astype(BF16)
    q = q * jnp.asarray(1.0 / math.sqrt(head), BF16)
    kv = jnp.dot(normed, wkv_ref[...], preferred_element_type=F32).astype(BF16)
    pair = 2 * head
    lane = lax.broadcasted_iota(jnp.int32, (cells, pair), 1)
    first = lane < head
    key = lax.broadcasted_iota(jnp.int32, (1, cells), 1)
    if len(parts) > 1:
        bias = jnp.where((key < cells // 2) & (valid_ref[0] == 0), -1e30, 0.0).astype(F32)
    else:
        bias = None
    for w in range(nw):
        at = slice(w * cells, (w + 1) * cells)
        for p in range(HEADS // 2):
            on = slice(p * pair, (p + 1) * pair)
            on_v = slice(width + p * pair, width + (p + 1) * pair)
            qp = q[at, on]
            zero = jnp.zeros_like(qp)
            q2 = jnp.concatenate([jnp.where(first, qp, zero), jnp.where(first, zero, qp)], axis=0)
            s = lax.dot_general(q2, kv[at, on], NT, preferred_element_type=F32)
            if bias is not None:
                s = s + bias
            e = jnp.exp(s - jnp.max(s, axis=-1, keepdims=True))
            e = (e * (1.0 / jnp.sum(e, axis=-1, keepdims=True))).astype(BF16)
            o = jnp.dot(e, kv[at, on_v], preferred_element_type=F32)
            att[at, on] = jnp.where(first, o[:cells], o[cells:]).astype(BF16)
    out = x + jnp.dot(att[...], wo_ref[...], preferred_element_type=F32)
    out = jnp.swapaxes(out.reshape(nw, rows, WIN, width), 0, 1).reshape(rows, cw, width).astype(BF16)
    for r in range(rows):
        lo[pl.ds(pl.multiple_of(r * cols + step * cw, cw), cw), :] = out[r]

    @pl.when(step == cols // cw - 1)
    def _():
        dec_ref[...] = lax.dot_general(wd_ref[...], lo[...], NT, preferred_element_type=F32).astype(BF16)


def window_layer(valid, gain, wq, wkv, wo, wd, *blocks):
    rows = sum(b.shape[0] for b in blocks)
    cols, width = blocks[0].shape[1:]
    cw = math.gcd(cols, 32)
    grid = (cols // cw,)
    tokens = rows * cols
    flops = 2 * tokens * width * (4 * width + wd.shape[0])
    return pl.pallas_call(
        functools.partial(layer_kernel, (rows, cols, cw)),
        grid=grid,
        out_shape=jax.ShapeDtypeStruct((wd.shape[0], tokens), BF16),
        in_specs=[
            pl.BlockSpec(memory_space=pltpu.SMEM),
            full_spec(gain.shape),
            full_spec(wq.shape),
            full_spec(wkv.shape),
            full_spec(wo.shape),
            full_spec(wd.shape),
        ]
        + [pl.BlockSpec((b.shape[0], cw, width), lambda i: (0, i, 0)) for b in blocks],
        out_specs=pl.BlockSpec((wd.shape[0], tokens), lambda i: (0, 0)),
        scratch_shapes=[
            pltpu.VMEM((rows * cw, width), BF16),
            pltpu.VMEM((tokens, width), BF16),
        ],
        cost_estimate=pl.CostEstimate(flops=flops * 2, bytes_accessed=12 * width * width, transcendentals=0),
        compiler_params=pltpu.CompilerParams(vmem_limit_bytes=60 * 2**20),
        name="window_layer",
    )(valid, gain, wq, wkv, wo, wd, *blocks)


def state_kernel(state_ref, nudge_ref, high_ref, low_ref, base_ref):
    rows, channels, length = state_ref.shape
    for y in range(0, rows, PATCH):
        s = state_ref[y : y + PATCH].reshape(PATCH * channels, length)
        s_high = s.astype(BF16)
        s_low = (s - s_high.astype(F32)).astype(BF16)
        kept = jnp.dot(s_high, high_ref[...], preferred_element_type=F32)
        kept = kept + jnp.dot(s_low, high_ref[...], preferred_element_type=F32)
        kept = kept + jnp.dot(s_high, low_ref[...], preferred_element_type=F32)
        kept = kept.reshape(PATCH, channels, length)
        base_ref[y : y + PATCH] = state_ref[y : y + PATCH] - nudge_ref[...][None] * kept


def decoded_kernel(base_ref, d0_ref, d1_ref, nudge_ref, high_ref, low_ref, out_ref):
    rows, channels, length = base_ref.shape
    cols = length // PATCH // 2
    part = PATCH * channels
    for r in range(rows // PATCH):
        pieces = []
        for b in range(PATCH):
            for d in (d0_ref, d1_ref):
                pieces.append(d[b * part : (b + 1) * part, r * cols : (r + 1) * cols])
        x = jnp.concatenate(pieces, axis=1)
        kept = jnp.dot(x, high_ref[...], preferred_element_type=F32)
        kept = kept + jnp.dot(x, low_ref[...], preferred_element_type=F32)
        kept = kept.reshape(PATCH, channels, length)
        y = r * PATCH
        out_ref[y : y + PATCH] = base_ref[y : y + PATCH] + nudge_ref[...][None] * kept


def tendency_row(south, centre, north):
    channels, length = centre.shape
    west = pltpu.roll(centre, 1, 1)
    east = pltpu.roll(centre, length - 1, 1)
    u = centre[:LEV][None]
    v = centre[LEV : 2 * LEV][None]
    dx = (east - west).reshape(VARS, LEV, length)
    dy = (north - south).reshape(VARS, LEV, length)
    advection = ((u * dx + v * dy) * 0.5).reshape(channels, length)
    return diffusion * (east + west + north + south - 4.0 * centre) - advection


def section_kernel(inside_ref, field_ref, before_ref, after_ref, out_ref, first):
    rows = field_ref.shape[0]

    def row(y):
        if y < 0:
            return before_ref[y + 2].astype(F32)
        if y >= rows:
            return after_ref[y - rows].astype(F32)
        return field_ref[y]

    for y in range(-1, rows + 1):
        value = row(y) + time_step * tendency_row(row(y - 1), row(y), row(y + 1))
        if y == -1:
            value = value * inside_ref[0]
        if y == rows:
            value = value * inside_ref[1]
        first[y + 1] = value
    for y in range(rows):
        second = tendency_row(first[y], first[y + 1], first[y + 2])
        out_ref[y] = 0.5 * (field_ref[y] + first[y + 1] + time_step * second)


def body(tokens, ln_gain, w_query, w_keyval, w_out, w_dec, nudge, state):
    half = WIN // 2
    tok_rows, tok_cols, width = tokens.shape
    n_lat, n_lon = lax.axis_size("lat"), lax.axis_size("lon")
    lat, lon = lax.axis_index("lat"), lax.axis_index("lon")
    channels = nudge.shape[0]
    length = state.shape[2] * n_lon
    band = state.shape[1] // n_lon
    lat_up = [(i, i + 1) for i in range(n_lat - 1)]
    swap = [(i, (i + 1) % n_lon) for i in range(n_lon)]

    raw_top = lax.ppermute(tokens[half:], "lat", lat_up)
    edge = lax.ppermute(tokens[:, :half], "lon", [(j, i) for i, j in swap])
    edge_top = lax.ppermute(edge[half:], "lat", lat_up)
    own = jnp.concatenate([tokens[:, half:], edge], axis=1)
    top = jnp.concatenate([raw_top[:, half:], edge_top], axis=1)

    wd = w_dec.reshape(width, channels, PATCH, PATCH).transpose(3, 2, 1, 0).reshape(-1, width)
    gain = ln_gain[None]
    valid = (lat > 0).astype(jnp.int32)[None]
    weights = (valid, gain, w_query, w_keyval, w_out, wd)

    is_low = lon == 0
    mine = jnp.where(is_low, state[:, :band], state[:, band:])
    other = jnp.where(is_low, state[:, band:], state[:, :band])
    other = lax.ppermute(other, "lon", swap)
    band_state = jnp.concatenate(
        [jnp.where(is_low, mine, other), jnp.where(is_low, other, mine)], axis=2
    ).transpose(1, 0, 2)
    high, low = filter_tables(length, KEEP)
    high, low = jnp.asarray(high), jnp.asarray(low)
    strength = nudge[:, None]
    field = jax.ShapeDtypeStruct((band, channels, length), F32)
    limit = pltpu.CompilerParams(vmem_limit_bytes=48 * 2**20)
    matmul = 2 * band * channels * length * length
    base = pl.pallas_call(
        state_kernel,
        out_shape=field,
        compiler_params=limit,
        cost_estimate=pl.CostEstimate(flops=3 * matmul, bytes_accessed=2**22, transcendentals=0),
        name="state_filter",
    )(band_state, strength, high, low)
    bottom_dec = window_layer(*weights, own[half:])

    dec = window_layer(*weights, top, own[:half])
    dec_top, dec_own = dec[:, : half * tok_cols], dec[:, half * tok_cols :]
    axes = ("lat", "lon")
    last_lon = n_lon - 1

    def flat(i, j):
        return i * n_lon + j

    to_last = [
        lax.ppermute(dec_top, axes, [(flat(i + 1, j), flat(i, last_lon)) for i in range(n_lat - 1)])
        for j in range(n_lon)
    ]
    across = lax.ppermute(jnp.where(is_low, bottom_dec, dec_own), "lon", swap)
    last = lat == n_lat - 1
    d0 = jnp.where(is_low, dec_own, jnp.where(last, across, to_last[0]))
    d1 = jnp.where(is_low, across, jnp.where(last, bottom_dec, to_last[1]))

    def decoder_rows(table):
        shaped = jnp.roll(table.reshape(-1, PATCH, length), -half, axis=0)
        return shaped.transpose(1, 0, 2).reshape(length, length)

    nudged = pl.pallas_call(
        decoded_kernel,
        out_shape=field,
        compiler_params=limit,
        cost_estimate=pl.CostEstimate(flops=2 * matmul, bytes_accessed=2**22, transcendentals=0),
        name="decoded_filter",
    )(base, d0, d1, strength, decoder_rows(high), decoder_rows(low))

    bands = n_lat * n_lon
    up = [(i, i + 1) for i in range(bands - 1)]
    down = [(j, i) for i, j in up]
    before = lax.ppermute(nudged[-2:].astype(BF16), axes, up)
    after = lax.ppermute(nudged[:2].astype(BF16), axes, down)
    place = lat * n_lon + lon
    inside = jnp.stack([place > 0, place < bands - 1]).astype(F32)
    advanced = pl.pallas_call(
        section_kernel,
        out_shape=field,
        in_specs=[pl.BlockSpec(memory_space=pltpu.SMEM)] + [pl.BlockSpec(memory_space=pltpu.VMEM)] * 3,
        scratch_shapes=[pltpu.VMEM((band + 2, channels, length), F32)],
        compiler_params=limit,
        name="two_sections",
    )(inside, nudged, before, after)
    return advanced.transpose(1, 0, 2)


def solution(mesh):
    in_specs = (
        P(("member", "lat"), "lon", None),
        P(),
        P(),
        P(),
        P(),
        P(),
        P(),
        P(None, ("member", "lat"), "lon"),
    )
    out_specs = P(None, ("member", "lat", "lon"), None)
    return jax.shard_map(body, mesh=mesh, in_specs=in_specs, out_specs=out_specs, check_vma=False)
```

time: 221 us -> 87.7 us (0.40)
  the two profiles are of different devices: /device:TPU:21 before, /device:TPU:15 now
where the time goes in v1:
time: 87.7 us; the launch traced here: 87.2 us
  Pallas kernels  37.7 us (43%)
  local copies, waits for them, and re-layouts  17.4 us (20%)
  starting transfers between devices  15.3 us (17%)
  waiting for transfers between devices  9.54 us (11%)
  other arithmetic  6.96 us (8%)
    pallas_call x2, Pallas kernels, window_layer(): pl.pallas_call(functools.partial(layer_kernel, (rows, cols, cw)), grid=gr...  30.2 us
    ppermute x2, waiting for transfers between devices, body(): lax.ppermute(dec_top, axes, [(flat(i + 1, j), flat(i, last_lon)) for i in...  5.18 us
    ppermute x1, waiting for transfers between devices, body(): after = lax.ppermute(nudged[:2].astype(BF16), axes, down)  4.34 us
    unnamed x19, local copies, waits for them, and re-layouts  3.8 us
    ppermute x2, starting transfers between devices, body(): lax.ppermute(dec_top, axes, [(flat(i + 1, j), flat(i, last_lon)) for i in...  3.6 us
    ppermute x1, starting transfers between devices, body(): edge_top = lax.ppermute(edge[half:], 'lat', lat_up)  3.15 us
    ppermute x1, starting transfers between devices, body(): raw_top = lax.ppermute(tokens[half:], 'lat', lat_up)  3.14 us
    pallas_call x1, Pallas kernels, body(): pl.pallas_call(decoded_kernel, out_shape=field, compiler_params=limit, co...  2.88 us
  transfers between devices with their start and end apart: 9, of which 3 were waited for; matrix products, arithmetic and copies ran while one was open for 22% of the time, Pallas kernels for 37%

profile of v1, /device:TPU:15, one launch (start us, length us, event | category | flops | bytes accessed | tf_op | source)
XLA Modules:
  0.0 87.2 jit_solution(17967483131291754341)
XLA Ops:
  0.0 1.0 %slice.73 = bf16[8,4,1024]{2,1,0:T(4,128)(2,1)S(1)} slice(bf16[8,96,1024]{2,1,0:T(8,128)(2,1)} %param.10), slice={[0:8], [0:4], [0:1024]} | slice | bytes 131072 | tf_op jit(solution)/shard_map/slice | solution.py:200
  1.0 0.7 collective-permute-start.2
  1.8 2.1 %slice.71 = bf16[4,96,1024]{2,1,0:T(8,128)(2,1)} slice(bf16[8,96,1024]{2,1,0:T(8,128)(2,1)} %param.10), slice={[4:8], [0:96], [0:1024]} | slice | bytes 1572864 | tf_op jit(solution)/shard_map/slice | solution.py:199
  3.9 3.1 %collective-permute-start.1 = (bf16[4,96,1024]{2,1,0:T(8,128)(2,1)}, bf16[4,96,1024]{2,1,0:T(8,128)(2,1)}, u32[]{:S(2)}, u32[]{:S(2)}) collective-permute-start(bf16[4,96,1024]{2,1,0:T(8,128)(2,1)} %slice.71), channel_id=1, source_target_pairs={{0,2},{2,4},{4,6},{6,8},{8,10},{10,12},{12,14},{1,3},{3,5},{5,7},{... | collective-permute-start | bytes 2359304 | tf_op jit(solution)/shard_map/ppermute | solution.py:199
  7.0 0.1 fusion.1
  7.1 1.3 %copy_select_fusion = f32[32,16,384]{2,0,1:T(8,128)} fusion(f32[32,16,384]{2,1,0:T(8,128)S(1)} %get-tuple-element.10, f32[32,16,384]{2,1,0:T(8,128)S(1)} %get-tuple-element.9, pred[]{:T(512)S(6)} %eq.6), kind=kLoop, calls=%fused_computation.6 | loop fusion | flops 196608 | bytes 2359297 | tf_op jit(solution)/shard_map/jit(_where)/select_n | solution.py:212
  8.5 0.3 collective-permute-start
  8.8 1.8 %slice.75 = bf16[8,92,1024]{2,1,0:T(8,128)(2,1)S(1)} slice(bf16[8,96,1024]{2,1,0:T(8,128)(2,1)} %param.10), slice={[0:8], [4:96], [0:1024]} | slice | bytes 3014656 | tf_op jit(solution)/shard_map/slice | solution.py:202
  10.6 2.3 %copy.20 = bf16[1024,512]{0,1:T(8,128)(2,1)} copy(bf16[1024,512]{1,0:T(8,128)(2,1)} %param.15) | data formatting | bytes 2097152 | tf_op args[5]
  12.9 2.2 %reshape.18 = bf16[1024,32,4,4]{0,3,2,1:T(4,128)(2,1)} reshape(bf16[1024,512]{0,1:T(8,128)(2,1)} %copy.20) | data formatting | bytes 2097152 | tf_op jit(solution)/shard_map/reshape | solution.py:205
  15.1 2.8 %copy.21 = bf16[4,4,32,1024]{3,2,1,0:T(8,128)(2,1)} copy(bf16[4,4,32,1024]{3,0,1,2:T(4,128)(2,1)} %bitcast.13) | data formatting | bytes 2097152 | tf_op jit(solution)/shard_map/transpose | solution.py:205
  18.0 3.1 %collective-permute-start.3 = (bf16[4,4,1024]{2,1,0:T(4,128)(2,1)S(1)}, bf16[4,4,1024]{2,1,0:T(4,128)(2,1)S(1)}, u32[]{:S(2)}, u32[]{:S(2)}) collective-permute-start(bf16[4,4,1024]{2,1,0:T(4,128)(2,1)S(1)} %slice.91), channel_id=1, source_target_pairs={{0,2},{2,4},{4,6},{6,8},{8,10},{10,12},{12,14},{1,3},{3,5},{5,7},{... | collective-permute-start | bytes 98312 | tf_op jit(solution)/shard_map/ppermute | solution.py:201
  21.2 1.4 %fusion = (bf16[4,96,1024]{2,1,0:T(8,128)(2,1)}, bf16[4,96,1024]{2,1,0:T(8,128)(2,1)}) fusion(bf16[8,92,1024]{2,1,0:T(8,128)(2,1)S(1)} %slice.75, bf16[8,4,1024]{2,1,0:T(4,128)(2,1)S(1)} %collective-permute-done.2), kind=kLoop, calls=%fused_computation.3 | loop fusion | flops 3145728 | bytes 3145728 | tf_op jit(solution)/shard_map/concatenate | solution.py:202
  22.6 12.2 %window_layer.3 = bf16[512,384]{1,0:T(8,128)(2,1)} custom-call(s32[1]{0:T(128)} %bitcast.4.valid_ref, f32[1,1024]{1,0:T(1,128)} %bitcast.17, bf16[1024,1024]{1,0:T(8,128)(2,1)} %wq_ref.3, bf16[1024,2048]{1,0:T(8,128)(2,1)} %wkv_ref.3, bf16[1024,1024]{1,0:T(8,128)(2,1)} %wo_ref.3, bf16[512,1024]{1,0:T(8,128)(2,1)} %bitcast.14, ...), custom_call_target="tpu_custom_call" | custom-call | flops 7247757312 | bytes 12582912 | tf_op jit(solution)/shard_map/window_layer/pallas_call | solution.py:100
  34.8 1.3 %slice.90 = bf16[4,92,1024]{2,1,0:T(8,128)(2,1)S(1)} slice(bf16[4,96,1024]{2,1,0:T(8,128)(2,1)} %collective-permute-done.1), slice={[0:4], [4:96], [0:1024]} | slice | bytes 1507328 | tf_op jit(solution)/shard_map/slice | solution.py:203
  36.2 1.0 %pad_maximum_fusion.1.rest_0_ = bf16[4,96,1024]{2,1,0:T(8,128)(2,1)} fusion(bf16[4,4,1024]{2,1,0:T(4,128)(2,1)S(1)} %collective-permute-done.3, bf16[4,92,1024]{2,1,0:T(8,128)(2,1)S(1)} %slice.90), kind=kLoop, calls=%fused_computation.5 | loop fusion | flops 1572864 | bytes 1572864 | tf_op jit(solution)/shard_map/concatenate | solution.py:203
  37.2 18.0 %window_layer.2 = bf16[512,768]{1,0:T(8,128)(2,1)} custom-call(s32[1]{0:T(128)} %bitcast.4.valid_ref, f32[1,1024]{1,0:T(1,128)} %bitcast.18, bf16[1024,1024]{1,0:T(8,128)(2,1)} %wq_ref.3, bf16[1024,2048]{1,0:T(8,128)(2,1)} %wkv_ref.3, bf16[1024,1024]{1,0:T(8,128)(2,1)} %wo_ref.3, bf16[512,1024]{1,0:T(8,128)(2,1)} %bitcast.15, ...), custom_call_target="tpu_custom_call" | custom-call | flops 14495514624 | bytes 12582912 | tf_op jit(solution)/shard_map/window_layer/pallas_call | solution.py:100
  55.1 1.2 %fusion.3 = (bf16[512,384]{1,0:T(8,128)(2,1)S(1)}, bf16[512,384]{1,0:T(8,128)(2,1)S(1)}) fusion(bf16[512,768]{1,0:T(8,128)(2,1)} %window_layer.2, bf16[512,384]{1,0:T(8,128)(2,1)S(1)} %copy-done.7, pred[]{:T(512)S(6)} %eq.6), kind=kLoop, calls=%fused_computation.16 | loop fusion | flops 196608 | bytes 1966081 | tf_op jit(solution)/shard_map/slice | solution.py:233
  56.3 1.3 %collective-permute-start.5 = (bf16[512,384]{1,0:T(8,128)(2,1)S(1)}, bf16[512,384]{1,0:T(8,128)(2,1)S(1)}, u32[]{:S(2)}, u32[]{:S(2)}) collective-permute-start(bf16[512,384]{1,0:T(8,128)(2,1)S(1)} %get-tuple-element.13), channel_id=1, source_target_pairs={{2,1},{4,3},{6,5},{8,7},{10,9},{12,11},{14,13},{18,17},{20,19},{22... | collective-permute-start | bytes 1179656 | tf_op jit(solution)/shard_map/ppermute | solution.py:241
  57.6 2.3 %collective-permute-start.6 = (bf16[512,384]{1,0:T(8,128)(2,1)S(1)}, bf16[512,384]{1,0:T(8,128)(2,1)S(1)}, u32[]{:S(2)}, u32[]{:S(2)}) collective-permute-start(bf16[512,384]{1,0:T(8,128)(2,1)S(1)} %get-tuple-element.13), channel_id=1, source_target_pairs={{3,1},{5,3},{7,5},{9,7},{11,9},{13,11},{15,13},{19,17},{21,19},{23... | collective-permute-start | bytes 1179656 | tf_op jit(solution)/shard_map/ppermute | solution.py:241
  60.0 1.6 %broadcast_select_fusion.2 = (f32[32,16,384]{2,0,1:T(8,128)S(1)}, f32[32,16,384]{2,0,1:T(8,128)S(1)}) fusion(f32[32,16,384]{2,0,1:T(8,128)} %collective-permute-done, pred[]{:T(512)S(6)} %eq.6, f32[32,16,384]{2,1,0:T(8,128)S(1)} %get-tuple-element.10, f32[32,16,384]{2,1,0:T(8,128)S(1)} %get-tuple-element.9), kind=kLoop, calls=%fused_computation.12 | loop fusion | flops 589824 | bytes 3932161 | tf_op jit(solution)/shard_map/jit(_where)/select_n | solution.py:215
  61.8 1.1 %copy-done.3 = bf16[768,768]{1,0:T(8,128)(2,1)S(1)} copy-done((bf16[768,768]{1,0:T(8,128)(2,1)S(1)}, bf16[768,768]{1,0:T(8,128)(2,1)}, u32[]{:S(2)}) %copy-start.3) | copy-done | bytes 1179672
  62.9 0.4 copy-done.4
  63.3 2.0 %state_filter.1.base_ref = f32[16,32,768]{2,1,0:T(8,128)S(1)} custom-call(f32[16,32,768]{2,1,0:T(8,128)S(1)} %maximum_bitcast_fusion.state_ref, f32[32,1]{1,0:T(8,128)S(1)} %copy.19.nudge_ref, bf16[768,768]{1,0:T(8,128)(2,1)S(1)} %copy-done.3, bf16[768,768]{1,0:T(8,128)(2,1)S(1)} %copy-done.4), custom_call_target="tpu_custom_call" | custom-call | flops 1811939328 | bytes 4194304 | tf_op jit(solution)/shard_map/state_filter/pallas_call | solution.py:223
  65.3 4.5 %collective-permute-done.5 = bf16[512,384]{1,0:T(8,128)(2,1)S(1)} collective-permute-done((bf16[512,384]{1,0:T(8,128)(2,1)S(1)}, bf16[512,384]{1,0:T(8,128)(2,1)S(1)}, u32[]{:S(2)}, u32[]{:S(2)}) %collective-permute-start.5) | collective-permute-done | bytes 393248 | tf_op jit(solution)/shard_map/ppermute | solution.py:241
  69.8 0.7 collective-permute-done.6
  70.7 2.9 %decoded_filter.1.field_ref = f32[16,32,768]{2,1,0:T(8,128)S(1)} custom-call(f32[16,32,768]{2,1,0:T(8,128)} %copy-done, bf16[512,384]{1,0:T(8,128)(2,1)S(1)} %get-tuple-element.16.d0_ref, bf16[512,384]{1,0:T(8,128)(2,1)S(1)} %get-tuple-element.15.d1_ref, f32[32,1]{1,0:T(8,128)S(1)} %copy.19.nudge_ref, bf16[768,768]{1,0:T(8,128)(2,1)S(1)} %copy-done.1, ...), custom_call_target="tpu_custom_call" | custom-call | flops 1207959552 | bytes 4194304 | tf_op jit(solution)/shard_map/decoded_filter/pallas_call | solution.py:253
  73.7 1.9 %collective-permute-start.7 = (bf16[2,32,768]{2,1,0:T(8,128)(2,1)S(1)}, bf16[2,32,768]{2,1,0:T(8,128)(2,1)S(1)}, u32[]{:S(2)}, u32[]{:S(2)}) collective-permute-start(bf16[2,32,768]{2,1,0:T(8,128)(2,1)S(1)} %get-tuple-element.12), channel_id=1, source_target_pairs={{0,1},{1,2},{2,3},{3,4},{4,5},{5,6},{6,7},{7,8},{8,9},{9,10},{10,1... | collective-permute-start | bytes 294920 | tf_op jit(solution)/shard_map/ppermute | solution.py:264
  75.6 2.4 %collective-permute-start.8 = (bf16[2,32,768]{2,1,0:T(8,128)(2,1)S(1)}, bf16[2,32,768]{2,1,0:T(8,128)(2,1)S(1)}, u32[]{:S(2)}, u32[]{:S(2)}) collective-permute-start(bf16[2,32,768]{2,1,0:T(8,128)(2,1)S(1)} %get-tuple-element.11), channel_id=1, source_target_pairs={{1,0},{2,1},{3,2},{4,3},{5,4},{6,5},{7,6},{8,7},{9,8},{10,9},{11,1... | collective-permute-start | bytes 294920 | tf_op jit(solution)/shard_map/ppermute | solution.py:265
  78.1 4.3 %collective-permute-done.8.after_ref = bf16[2,32,768]{2,1,0:T(8,128)(2,1)S(1)} collective-permute-done((bf16[2,32,768]{2,1,0:T(8,128)(2,1)S(1)}, bf16[2,32,768]{2,1,0:T(8,128)(2,1)S(1)}, u32[]{:S(2)}, u32[]{:S(2)}) %collective-permute-start.8) | collective-permute-done | bytes 98336 | tf_op jit(solution)/shard_map/ppermute | solution.py:265
  82.4 2.6 %two_sections.1 = f32[16,32,768]{2,1,0:T(8,128)S(1)} custom-call(f32[2]{0:T(128)S(1)} %add_convert_fusion.inside_ref, f32[16,32,768]{2,1,0:T(8,128)S(1)} %decoded_filter.1.field_ref, bf16[2,32,768]{2,1,0:T(8,128)(2,1)S(1)} %collective-permute-done.7.before_ref, bf16[2,32,768]{2,1,0:T(8,128)(2,1)S(1)} %collective-permute-done.8.after_ref), custom_call_target="tpu_custom_call" | custom-call | tf_op jit(solution)/shard_map/two_sections/pallas_call | solution.py:268
  85.1 2.1 %copy.23 = f32[32,16,768]{2,1,0:T(8,128)} copy(f32[32,16,768]{2,0,1:T(8,128)S(1)} %bitcast.12) | data formatting | bytes 3145728 | tf_op jit(solution)/shard_map/transpose | solution.py:276
  (30 shorter events, 0.6 us)
Async XLA Ops:
  0.0 7.0 %copy-start.6 = (f32[32,32,384]{2,1,0:T(8,128)S(1)}, f32[32,32,384]{2,1,0:T(8,128)}, u32[]{:S(2)}) copy-start(f32[32,32,384]{2,1,0:T(8,128)} %param.17) | copy-start | bytes 4718596
  1.0 17.0 %collective-permute-start.2 = (bf16[8,4,1024]{2,1,0:T(4,128)(2,1)S(1)}, bf16[8,4,1024]{2,1,0:T(4,128)(2,1)S(1)}, u32[]{:S(2)}, u32[]{:S(2)}) collective-permute-start(bf16[8,4,1024]{2,1,0:T(4,128)(2,1)S(1)} %slice.73), channel_id=1, source_target_pairs={{1,0},{0,1},{3,2},{2,3},{5,4},{4,5},{7,6},{6,7},{9,8},{8,9},{11,10... | collective-permute-start | bytes 196616 | tf_op jit(solution)/shard_map/ppermute | solution.py:200
  3.9 31.0 %collective-permute-start.1 = (bf16[4,96,1024]{2,1,0:T(8,128)(2,1)}, bf16[4,96,1024]{2,1,0:T(8,128)(2,1)}, u32[]{:S(2)}, u32[]{:S(2)}) collective-permute-start(bf16[4,96,1024]{2,1,0:T(8,128)(2,1)} %slice.71), channel_id=1, source_target_pairs={{0,2},{2,4},{4,6},{6,8},{8,10},{10,12},{12,14},{1,3},{3,5},{5,7},{... | collective-permute-start | bytes 2359304 | tf_op jit(solution)/shard_map/ppermute | solution.py:199
  8.5 51.5 %collective-permute-start = (f32[32,16,384]{2,0,1:T(8,128)}, f32[32,16,384]{2,0,1:T(8,128)}, u32[]{:S(2)}, u32[]{:S(2)}) collective-permute-start(f32[32,16,384]{2,0,1:T(8,128)} %copy_select_fusion), channel_id=1, source_target_pairs={{0,1},{1,0},{2,3},{3,2},{4,5},{5,4},{6,7},{7,6},{8,9},{9,8},{10,11... | collective-permute-start | bytes 2359304 | tf_op jit(solution)/shard_map/ppermute | solution.py:213
  15.1 2.8 %copy-start.8 = (f32[32]{0:T(128)S(1)}, f32[32]{0:T(128)}, u32[]{:S(2)}) copy-start(f32[32]{0:T(128)} %param.16) | copy-start | bytes 388
  18.0 18.1 %collective-permute-start.3 = (bf16[4,4,1024]{2,1,0:T(4,128)(2,1)S(1)}, bf16[4,4,1024]{2,1,0:T(4,128)(2,1)S(1)}, u32[]{:S(2)}, u32[]{:S(2)}) collective-permute-start(bf16[4,4,1024]{2,1,0:T(4,128)(2,1)S(1)} %slice.91), channel_id=1, source_target_pairs={{0,2},{2,4},{4,6},{6,8},{8,10},{10,12},{12,14},{1,3},{3,5},{5,7},{... | collective-permute-start | bytes 98312 | tf_op jit(solution)/shard_map/ppermute | solution.py:201
  37.2 18.0 %copy-start.7 = (bf16[512,384]{1,0:T(8,128)(2,1)S(1)}, bf16[512,384]{1,0:T(8,128)(2,1)}, u32[]{:S(2)}) copy-start(bf16[512,384]{1,0:T(8,128)(2,1)} %window_layer.3) | copy-start | bytes 1179652
  56.3 13.5 %collective-permute-start.5 = (bf16[512,384]{1,0:T(8,128)(2,1)S(1)}, bf16[512,384]{1,0:T(8,128)(2,1)S(1)}, u32[]{:S(2)}, u32[]{:S(2)}) collective-permute-start(bf16[512,384]{1,0:T(8,128)(2,1)S(1)} %get-tuple-element.13), channel_id=1, source_target_pairs={{2,1},{4,3},{6,5},{8,7},{10,9},{12,11},{14,13},{18,17},{20,19},{22... | collective-permute-start | bytes 1179656 | tf_op jit(solution)/shard_map/ppermute | solution.py:241
  57.6 12.9 %collective-permute-start.6 = (bf16[512,384]{1,0:T(8,128)(2,1)S(1)}, bf16[512,384]{1,0:T(8,128)(2,1)S(1)}, u32[]{:S(2)}, u32[]{:S(2)}) collective-permute-start(bf16[512,384]{1,0:T(8,128)(2,1)S(1)} %get-tuple-element.13), channel_id=1, source_target_pairs={{3,1},{5,3},{7,5},{9,7},{11,9},{13,11},{15,13},{19,17},{21,19},{23... | collective-permute-start | bytes 1179656 | tf_op jit(solution)/shard_map/ppermute | solution.py:241
  59.9 10.6 %collective-permute-start.4 = (bf16[512,384]{1,0:T(8,128)(2,1)S(1)}, bf16[512,384]{1,0:T(8,128)(2,1)S(1)}, u32[]{:S(2)}, u32[]{:S(2)}) collective-permute-start(bf16[512,384]{1,0:T(8,128)(2,1)S(1)} %get-tuple-element.14), channel_id=1, source_target_pairs={{0,1},{1,0},{2,3},{3,2},{4,5},{5,4},{6,7},{7,6},{8,9},{9,8},{10,11... | collective-permute-start | bytes 1179656 | tf_op jit(solution)/shard_map/ppermute | solution.py:244
  61.6 1.3 %copy-start.3 = (bf16[768,768]{1,0:T(8,128)(2,1)S(1)}, bf16[768,768]{1,0:T(8,128)(2,1)}, u32[]{:S(2)}) copy-start(bf16[768,768]{1,0:T(8,128)(2,1)} %constant.20.clone.high_ref) | copy-start | bytes 3538948
  61.7 1.6 %copy-start.4 = (bf16[768,768]{1,0:T(8,128)(2,1)S(1)}, bf16[768,768]{1,0:T(8,128)(2,1)}, u32[]{:S(2)}) copy-start(bf16[768,768]{1,0:T(8,128)(2,1)} %constant.21.clone.low_ref) | copy-start | bytes 3538948
  63.3 7.2 %copy-start.5 = (bf16[512,768]{1,0:T(8,128)(2,1)S(1)}, bf16[512,768]{1,0:T(8,128)(2,1)}, u32[]{:S(2)}) copy-start(bf16[512,768]{1,0:T(8,128)(2,1)} %window_layer.2) | copy-start | bytes 2359300
  65.3 5.3 %copy-start = (f32[16,32,768]{2,1,0:T(8,128)}, f32[16,32,768]{2,1,0:T(8,128)S(1)}, u32[]{:S(2)}) copy-start(f32[16,32,768]{2,1,0:T(8,128)S(1)} %state_filter.1.base_ref) | copy-start | bytes 4718596
  65.3 5.3 %copy-start.1 = (bf16[768,768]{1,0:T(8,128)(2,1)S(1)}, bf16[768,768]{1,0:T(8,128)(2,1)}, u32[]{:S(2)}) copy-start(bf16[768,768]{1,0:T(8,128)(2,1)} %constant.29.high_ref) | copy-start | bytes 3538948
  65.3 5.3 %copy-start.2 = (bf16[768,768]{1,0:T(8,128)(2,1)S(1)}, bf16[768,768]{1,0:T(8,128)(2,1)}, u32[]{:S(2)}) copy-start(bf16[768,768]{1,0:T(8,128)(2,1)} %constant.36.low_ref) | copy-start | bytes 3538948
  73.7 4.4 %collective-permute-start.7 = (bf16[2,32,768]{2,1,0:T(8,128)(2,1)S(1)}, bf16[2,32,768]{2,1,0:T(8,128)(2,1)S(1)}, u32[]{:S(2)}, u32[]{:S(2)}) collective-permute-start(bf16[2,32,768]{2,1,0:T(8,128)(2,1)S(1)} %get-tuple-element.12), channel_id=1, source_target_pairs={{0,1},{1,2},{2,3},{3,4},{4,5},{5,6},{6,7},{7,8},{8,9},{9,10},{10,1... | collective-permute-start | bytes 294920 | tf_op jit(solution)/shard_map/ppermute | solution.py:264
  75.6 6.8 %collective-permute-start.8 = (bf16[2,32,768]{2,1,0:T(8,128)(2,1)S(1)}, bf16[2,32,768]{2,1,0:T(8,128)(2,1)S(1)}, u32[]{:S(2)}, u32[]{:S(2)}) collective-permute-start(bf16[2,32,768]{2,1,0:T(8,128)(2,1)S(1)} %get-tuple-element.11), channel_id=1, source_target_pairs={{1,0},{2,1},{3,2},{4,3},{5,4},{6,5},{7,6},{8,7},{9,8},{10,9},{11,1... | collective-permute-start | bytes 294920 | tf_op jit(solution)/shard_map/ppermute | solution.py:265

commit v2 on v0

v2 whole, which is shorter than its diff:
```python
import functools
import math

import jax
import jax.numpy as jnp
import numpy as np
from jax import lax
from jax.experimental import pallas as pl
from jax.experimental.pallas import tpu as pltpu
from jax.sharding import PartitionSpec as P

HEADS = 16
WIN = 8
PATCH = 4
VARS = 4
LEV = 8
KEEP = 256

time_step = 0.1
diffusion = 0.5
epsilon = 1e-05
F32 = jnp.float32
BF16 = jnp.bfloat16
NT = (((1,), (1,)), ((), ()))


def filter_rows(length, kept, stride):
    offset = np.arange(length)
    waves = np.arange(1, kept)
    angles = 2.0 * np.pi * ((offset[:, None] * waves[None, :]) % length) / length
    kernel = (1.0 + 2.0 * np.cos(angles).sum(1)) / length
    return kernel[(offset[None, :] - stride * np.arange(16)[:, None]) % length].astype(np.float32)


def split(value):
    high = value.astype(BF16)
    return high, (value - high.astype(F32)).astype(BF16)


def cycle_kernel(
    n_lat, tokens, state, wq_hbm, wkv_hbm, wo_hbm, wd_hbm, gain_ref, nudge_ref, rows1_ref, rows4_ref, out_ref,
    wqkv, wo, wd, wdt, own, recv, edge, corner, xs, xs_b, normed, qkv, qkv_b, att, lo,
    band, base, high, low, dhigh, dlow, d0, d1, send_top, send_side, up_rows, down_rows, before, after, first,
    load_sem, send_sem, recv_sem,
):
    lat, lon = lax.axis_index("lat"), lax.axis_index("lon")
    half = WIN // 2
    cols, width = tokens.shape[1:]
    windows = cols // WIN
    strip = edge.shape[1]
    tall, channels, length = base.shape
    wide = state.shape[2]
    is_low, is_high = lon == 0, lon == 1
    has_prev, has_next = lat > 0, lat < n_lat - 1
    prev, nxt = jnp.maximum(lat - 1, 0), jnp.minimum(lat + 1, n_lat - 1)
    peer = 1 - lon

    def load(i, src, dst):
        return pltpu.make_async_copy(src, dst, load_sem.at[i])

    def remote(i, src, dst, to_lat, to_lon):
        return pltpu.make_async_remote_copy(
            src_ref=src, dst_ref=dst, send_sem=send_sem.at[i], recv_sem=recv_sem.at[i],
            device_id={"lat": to_lat, "lon": to_lon}, device_id_type=pl.DeviceIdType.MESH,
        )

    own_load = load(0, tokens, own)
    loads = [
        load(1, wq_hbm, wqkv.at[:, pl.ds(0, width)]),
        load(2, wkv_hbm, wqkv.at[:, pl.ds(width, 2 * width)]),
        load(3, wo_hbm, wo),
        load(4, wd_hbm, wd),
    ]
    my_rows = pl.ds(pl.multiple_of(lon * tall, 8), tall)
    peer_rows = pl.ds(pl.multiple_of(peer * tall, 8), tall)
    my_cols = pl.ds(pl.multiple_of(lon * wide, 128), wide)
    own_state = load(5, state.at[:, my_rows, :], band.at[:, :, my_cols])
    own_load.start()
    for item in loads:
        item.start()
    own_state.start()

    barrier = pltpu.get_barrier_semaphore()

    def greet(to_lat, to_lon):
        pl.semaphore_signal(
            barrier, inc=1, device_id={"lat": to_lat, "lon": to_lon}, device_id_type=pl.DeviceIdType.MESH
        )

    greet(lat, peer)

    @pl.when(has_prev)
    def _():
        greet(prev, lon)
        greet(prev, peer)

    @pl.when(has_next)
    def _():
        greet(nxt, lon)
        greet(nxt, peer)

    pl.semaphore_wait(barrier, 1 + 2 * has_prev.astype(jnp.int32) + 2 * has_next.astype(jnp.int32))

    row_a = remote(0, tokens.at[pl.ds(half, half), pl.ds(0, strip), :], recv.at[:, pl.ds(0, strip), :], nxt, lon)
    row_b = remote(
        1, tokens.at[pl.ds(half, half), pl.ds(strip, cols - strip), :],
        recv.at[:, pl.ds(strip, cols - strip), :], nxt, lon,
    )
    edge_copy = remote(2, tokens.at[:, pl.ds(0, strip), :], edge, lat, peer)
    state_copy = remote(3, state.at[:, peer_rows, :], band.at[:, :, my_cols], lat, peer)
    corner_copy = remote(4, recv.at[:, pl.ds(0, strip), :], corner, lat, peer)

    @pl.when(has_next)
    def _():
        row_a.start()
        row_b.start()

    edge_copy.start()
    state_copy.start()

    def project(block, strip_block, x_out, qkv_out, at):
        for r in range(half):
            row = block[r].astype(F32)
            side = strip_block[r].astype(F32)
            row = jnp.concatenate([row[half:], side[:half]], axis=0)
            centred = row - jnp.mean(row, axis=-1, keepdims=True)
            variance = jnp.mean(centred * centred, axis=-1, keepdims=True)
            unit = centred * lax.rsqrt(variance + epsilon) * gain_ref[...]
            x_out[r] = row.reshape(windows, WIN, width)
            normed[r] = unit.reshape(windows, WIN, width)
        flat = jnp.swapaxes(normed[...], 0, 1).reshape(windows * half * WIN, width).astype(BF16)
        scale = jnp.float32(1.0 / math.sqrt(width // HEADS))

        @pl.loop(0, 3 * width // 256)
        def _(n):
            on = pl.ds(pl.multiple_of(n * 256, 256), 256)
            value = jnp.dot(flat, wqkv[:, on], preferred_element_type=F32).astype(BF16)
            value = (value.astype(F32) * jnp.where(n < width // 256, scale, 1.0)).astype(BF16)
            qkv_out[:, at, on] = value.reshape(windows, half * WIN, 256)

    def attend(qkv_in, cells, bias):
        head = width // HEADS
        pair = 2 * head
        lanes = lax.broadcasted_iota(jnp.int32, (cells, pair), 1) < head

        @pl.loop(0, windows)
        def _(w):
            for p in range(HEADS // 2):
                on = p * pair
                qp = qkv_in[w, :, on : on + pair]
                zero = jnp.zeros_like(qp)
                q2 = jnp.concatenate([jnp.where(lanes, qp, zero), jnp.where(lanes, zero, qp)], axis=0)
                kp = qkv_in[w, :, width + on : width + on + pair]
                vp = qkv_in[w, :, 2 * width + on : 2 * width + on + pair]
                s = lax.dot_general(q2, kp, NT, preferred_element_type=F32)
                if bias is not None:
                    s = s + bias
                e = jnp.exp(s - jnp.max(s, axis=-1, keepdims=True))
                e = (e * (1.0 / jnp.sum(e, axis=-1, keepdims=True))).astype(BF16)
                o = jnp.dot(e, vp, preferred_element_type=F32)
                att[w, 0:cells, on : on + pair] = jnp.where(lanes, o[:cells], o[cells:]).astype(BF16)

    def decode(at, x_in, outs):
        mixed = att[:, at, :].reshape(windows * half * WIN, width)

        @pl.loop(0, width // 256)
        def _(n):
            on = pl.ds(pl.multiple_of(n * 256, 256), 256)
            update = jnp.dot(mixed, wo[:, on], preferred_element_type=F32)
            update = jnp.swapaxes(update.reshape(windows, half, WIN, 256), 0, 1)
            value = x_in[:, :, :, on] + update
            lo[:, on] = value.reshape(half * cols, 256).astype(BF16)

        value = lax.dot_general(wdt[...], lo[...], NT, preferred_element_type=F32).astype(BF16)
        for chosen_here, out in outs:
            if chosen_here is None:
                out[...] = value
            else:

                @pl.when(chosen_here)
                def _():
                    out[...] = value

    top_at, own_at = slice(0, half * WIN), slice(half * WIN, 2 * half * WIN)
    x_top, x_own = xs.at[0], xs.at[1]
    own_load.wait()
    edge_copy.wait()
    loads[0].wait()
    loads[1].wait()
    project(own.at[pl.ds(0, half)], edge.at[pl.ds(0, half)], x_own, qkv, own_at)

    loads[2].wait()
    loads[3].wait()
    patches = wdt.shape[0]
    row_id = lax.broadcasted_iota(jnp.int32, (patches, patches), 0)
    col_id = lax.broadcasted_iota(jnp.int32, (patches, patches), 1)
    area = PATCH * PATCH
    wanted = (row_id % channels) * area + (row_id // channels) % PATCH * PATCH + row_id // (PATCH * channels)
    chosen = (col_id == wanted).astype(F32).astype(BF16)
    wdt[...] = lax.dot_general(chosen, wd[...], NT, preferred_element_type=F32).astype(BF16)

    @pl.when(lat == n_lat - 1)
    def _():
        project(own.at[pl.ds(half, half)], edge.at[pl.ds(half, half)], xs_b, qkv_b, top_at)
        attend(qkv_b, half * WIN, None)
        decode(top_at, xs_b, [(is_high, d1), (is_low, send_side)])

    blocks = length // 16

    @pl.loop(0, blocks)
    def _(g):
        on = pl.ds(pl.multiple_of(g * 16, 16), 16)
        high[on, :], low[on, :] = split(pltpu.roll(rows1_ref[...], g * 16, 1))
        per = blocks // PATCH
        shift = lax.rem((lax.rem(g, per) * 16 + half) * PATCH + g // per, length)
        dhigh[on, :], dlow[on, :] = split(pltpu.roll(rows4_ref[...], shift, 1))

    own_state.wait()
    state_copy.wait()

    @pl.loop(0, channels // LEV)
    def _(g):
        on = pl.ds(pl.multiple_of(g * LEV, LEV), LEV)
        s = band[on].reshape(LEV * tall, length)
        s_high, s_low = split(s)
        kept = jnp.dot(s_high, high[...], preferred_element_type=F32)
        kept = kept + jnp.dot(s_low, high[...], preferred_element_type=F32)
        kept = kept + jnp.dot(s_high, low[...], preferred_element_type=F32)
        kept = s.reshape(LEV, tall, length) - nudge_ref[on][:, :, None] * kept.reshape(LEV, tall, length)
        base[:, on, :] = jnp.swapaxes(kept, 0, 1)

    @pl.when(lat == 0)
    def _():
        recv[...] = jnp.zeros_like(recv)

    @pl.when(has_prev)
    def _():
        row_a.wait_recv()

    corner_copy.start()

    @pl.when(has_prev)
    def _():
        row_b.wait_recv()

    corner_copy.wait()
    project(recv, corner, x_top, qkv, top_at)
    key = lax.broadcasted_iota(jnp.int32, (1, 2 * half * WIN), 1)
    bias = jnp.where((key < half * WIN) & (lat == 0), -1e30, 0.0).astype(F32)
    attend(qkv, 2 * half * WIN, bias)

    top_copies = [remote(5 + j, send_top, d, prev, 1) for j, d in enumerate((d0, d1))]
    side_high = is_low & (lat == n_lat - 1)

    decode(top_at, x_top, [(None, send_top)])
    for j in range(2):

        @pl.when(has_prev & (lon == j))
        def _():
            top_copies[j].start()

    @pl.when(side_high)
    def _():
        to_high_last = remote(7, send_side, d0, lat, 1)
        to_high_last.start()

    decode(own_at, x_own, [(is_high, send_side), (is_low, d0)])

    @pl.when(is_high)
    def _():
        to_low_now = remote(8, send_side, d1, lat, 0)
        to_low_now.start()

    @pl.when(is_low)
    def _():
        remote(8, send_side, d1, lat, peer).wait_recv()

    @pl.when(is_high & has_next)
    def _():
        remote(5, send_top, d0, prev, 1).wait_recv()
        remote(6, send_top, d1, prev, 1).wait_recv()

    @pl.when(is_high & (lat == n_lat - 1))
    def _():
        remote(7, send_side, d0, lat, peer).wait_recv()

    part = PATCH * channels

    def nudge_rows(r):
        pieces = []
        for b in range(PATCH):
            for d in (d0, d1):
                pieces.append(d[b * part : (b + 1) * part, r * cols : (r + 1) * cols])
        x = jnp.concatenate(pieces, axis=1)
        kept = jnp.dot(x, dhigh[...], preferred_element_type=F32)
        kept = kept + jnp.dot(x, dlow[...], preferred_element_type=F32)
        y = r * PATCH
        base[y : y + PATCH] = base[y : y + PATCH] + nudge_ref[...][None] * kept.reshape(PATCH, channels, length)

    up_lat, up_lon = jnp.where(is_low, lat, nxt), peer
    down_lat, down_lon = jnp.where(is_low, prev, lat), peer
    inside_up, inside_down = is_low | has_next, is_high | has_prev
    up_copy = remote(9, up_rows, before, up_lat, up_lon)
    down_copy = remote(10, down_rows, after, down_lat, down_lon)
    count = tall // PATCH
    nudge_rows(count - 1)
    up_rows[...] = base[tall - 2 : tall].astype(BF16)

    @pl.when(inside_up)
    def _():
        up_copy.start()

    nudge_rows(0)
    down_rows[...] = base[0:2].astype(BF16)

    @pl.when(inside_down)
    def _():
        down_copy.start()

    for r in range(1, count - 1):
        nudge_rows(r)

    def row(y):
        if y < 0:
            return before[y + 2].astype(F32)
        if y >= tall:
            return after[y - tall].astype(F32)
        return base[y]

    def section(y):
        first[y + 1] = row(y) + time_step * tendency_row(row(y - 1), row(y), row(y + 1))

    @pl.loop(1, tall - 1)
    def _(y):
        first[y + 1] = base[y] + time_step * tendency_row(base[y - 1], base[y], base[y + 1])

    @pl.when(inside_down)
    def _():
        up_copy.wait_recv()

    @pl.when(jnp.logical_not(inside_down))
    def _():
        before[...] = jnp.zeros_like(before)

    @pl.when(inside_up)
    def _():
        down_copy.wait_recv()

    @pl.when(jnp.logical_not(inside_up))
    def _():
        after[...] = jnp.zeros_like(after)

    for y in (-1, 0, tall - 1, tall):
        section(y)
    first[0] = first[0] * jnp.where(inside_down, 1.0, 0.0)
    first[tall + 1] = first[tall + 1] * jnp.where(inside_up, 1.0, 0.0)

    @pl.loop(0, tall)
    def _(y):
        second = tendency_row(first[y], first[y + 1], first[y + 2])
        out_ref[y] = 0.5 * (base[y] + first[y + 1] + time_step * second)

    @pl.when(has_next)
    def _():
        row_a.wait_send()
        row_b.wait_send()

    for j in range(2):

        @pl.when(has_prev & (lon == j))
        def _():
            top_copies[j].wait_send()

    @pl.when(side_high)
    def _():
        remote(7, send_side, d0, lat, 1).wait_send()

    @pl.when(is_high)
    def _():
        remote(8, send_side, d1, lat, 0).wait_send()

    @pl.when(inside_up)
    def _():
        up_copy.wait_send()

    @pl.when(inside_down)
    def _():
        down_copy.wait_send()


def body(sizes, tokens, ln_gain, w_query, w_keyval, w_out, w_dec, nudge, state):
    half = WIN // 2
    cols, width = tokens.shape[1:]
    channels = nudge.shape[0]
    length = state.shape[2] * sizes["lon"]
    tall = state.shape[1] // sizes["lon"]
    windows = cols // WIN
    patches = w_dec.shape[1]
    strip = 16
    cells = half * WIN
    hbm, vmem = pl.BlockSpec(memory_space=pl.ANY), pl.BlockSpec(memory_space=pltpu.VMEM)
    V = pltpu.VMEM
    field = (tall, channels, length)
    flow = (patches, half * cols)
    scratch = [
        V((width, 3 * width), BF16), V((width, width), BF16), V(w_dec.shape, BF16), V((patches, width), BF16),
        V(tokens.shape, BF16), V((half, cols, width), BF16), V((2 * half, strip, width), BF16),
        V((half, strip, width), BF16),
        V((2, half, windows, WIN, width), F32), V((half, windows, WIN, width), F32),
        V((half, windows, WIN, width), F32),
        V((windows, 2 * cells, 3 * width), BF16), V((windows, cells, 3 * width), BF16),
        V((windows, 2 * cells, width), BF16), V((half * cols, width), BF16),
        V((channels, tall, length), F32), V(field, F32),
        V((length, length), BF16), V((length, length), BF16), V((length, length), BF16), V((length, length), BF16),
        V(flow, BF16), V(flow, BF16), V(flow, BF16), V(flow, BF16),
        V((2, channels, length), BF16), V((2, channels, length), BF16),
        V((2, channels, length), BF16), V((2, channels, length), BF16),
        V((tall + 2, channels, length), F32),
        pltpu.SemaphoreType.DMA((6,)), pltpu.SemaphoreType.DMA((11,)), pltpu.SemaphoreType.DMA((11,)),
    ]
    advanced = pl.pallas_call(
        functools.partial(cycle_kernel, sizes["lat"]),
        out_shape=jax.ShapeDtypeStruct(field, F32),
        in_specs=[hbm] * 6 + [vmem] * 4,
        out_specs=vmem,
        scratch_shapes=scratch,
        compiler_params=pltpu.CompilerParams(
            collective_id=0, has_side_effects=True, vmem_limit_bytes=62 * 2**20
        ),
        name="cycle",
    )(
        tokens, state, w_query, w_keyval, w_out, w_dec, ln_gain[None], nudge[:, None],
        jnp.asarray(filter_rows(length, KEEP, 1)), jnp.asarray(filter_rows(length, KEEP, PATCH)),
    )
    return advanced.transpose(1, 0, 2)


def tendency_row(south, centre, north):
    channels, length = centre.shape
    west = pltpu.roll(centre, 1, 1)
    east = pltpu.roll(centre, length - 1, 1)
    u = centre[:LEV][None]
    v = centre[LEV : 2 * LEV][None]
    dx = (east - west).reshape(VARS, LEV, length)
    dy = (north - south).reshape(VARS, LEV, length)
    advection = ((u * dx + v * dy) * 0.5).reshape(channels, length)
    return diffusion * (east + west + north + south - 4.0 * centre) - advection


def solution(mesh):
    in_specs = (
        P(("member", "lat"), "lon", None),
        P(),
        P(),
        P(),
        P(),
        P(),
        P(),
        P(None, ("member", "lat"), "lon"),
    )
    out_specs = P(None, ("member", "lat", "lon"), None)
    return jax.shard_map(
        functools.partial(body, dict(mesh.shape)),
        mesh=mesh,
        in_specs=in_specs,
        out_specs=out_specs,
        check_vma=False,
    )
```

time: 221 us -> 78.9 us (0.36)
  the two profiles are of different devices: /device:TPU:21 before, /device:TPU:27 now
where the time goes in v2:
time: 78.9 us; the launch traced here: 78.7 us
  Pallas kernels  73.9 us (94%)
  local copies, waits for them, and re-layouts  4.8 us (6%)
    pallas_call x1, Pallas kernels, body(): pl.pallas_call(functools.partial(cycle_kernel, sizes['lat']), out_shape=j...  73.9 us
    transpose x1, local copies, waits for them, and re-layouts, body(): return advanced.transpose(1, 0, 2)  3.46 us

profile of v2, /device:TPU:27, one launch (start us, length us, event | category | flops | bytes accessed | tf_op | source)
XLA Modules:
  0.0 78.7 jit_solution(15447976972169046669)
XLA Ops:
  0.0 1.3 %copy.11.nudge_ref = f32[32,1]{1,0:T(8,128)} copy(f32[32,1]{0,1:T(1,128)} %bitcast.5) | data formatting | bytes 256 | tf_op jit(solution)/shard_map/broadcast_in_dim | solution.py:432
  1.3 73.9 %cycle.1 = f32[16,32,768]{2,1,0:T(8,128)} custom-call(bf16[8,96,1024]{2,1,0:T(8,128)(2,1)} %tokens.1, f32[32,32,384]{2,1,0:T(8,128)} %state.1, bf16[1024,1024]{1,0:T(8,128)(2,1)} %wq_hbm.1, bf16[1024,2048]{1,0:T(8,128)(2,1)} %wkv_hbm.1, bf16[1024,1024]{1,0:T(8,128)(2,1)} %wo_hbm.1, bf16[1024,512]{1,0:T(8,128)(2,1)} %wd_hbm.1, f32[1,1024]{1,0:T(1,128)} %bitcast.4, ...), custom_call_target="tpu_custom_call" | custom-call | tf_op jit(solution)/shard_map/cycle/pallas_call | solution.py:421
  75.3 3.5 %copy.12 = f32[32,16,768]{2,1,0:T(8,128)} copy(f32[32,16,768]{2,0,1:T(8,128)} %bitcast.3) | data formatting | bytes 3145728 | tf_op jit(solution)/shard_map/transpose | solution.py:435

commit v3 on v2

--- a/solution.py
+++ b/solution.py
@@ -145,20 +145,27 @@
 
         @pl.loop(0, windows)
         def _(w):
-            for p in range(HEADS // 2):
-                on = p * pair
-                qp = qkv_in[w, :, on : on + pair]
-                zero = jnp.zeros_like(qp)
-                q2 = jnp.concatenate([jnp.where(lanes, qp, zero), jnp.where(lanes, zero, qp)], axis=0)
-                kp = qkv_in[w, :, width + on : width + on + pair]
-                vp = qkv_in[w, :, 2 * width + on : 2 * width + on + pair]
-                s = lax.dot_general(q2, kp, NT, preferred_element_type=F32)
-                if bias is not None:
-                    s = s + bias
-                e = jnp.exp(s - jnp.max(s, axis=-1, keepdims=True))
-                e = (e * (1.0 / jnp.sum(e, axis=-1, keepdims=True))).astype(BF16)
-                o = jnp.dot(e, vp, preferred_element_type=F32)
-                att[w, 0:cells, on : on + pair] = jnp.where(lanes, o[:cells], o[cells:]).astype(BF16)
+            for group in range(0, HEADS // 2, 4):
+                spots = [p * pair for p in range(group, group + 4)]
+                scores = []
+                for on in spots:
+                    qp = qkv_in[w, :, on : on + pair]
+                    zero = jnp.zeros_like(qp)
+                    q2 = jnp.concatenate([jnp.where(lanes, qp, zero), jnp.where(lanes, zero, qp)], axis=0)
+                    kp = qkv_in[w, :, width + on : width + on + pair]
+                    s = lax.dot_general(q2, kp, NT, preferred_element_type=F32)
+                    scores.append(s if bias is None else s + bias)
+                peaks = [jnp.max(s, axis=-1, keepdims=True) for s in scores]
+                powers = [jnp.exp(s - m).astype(BF16) for s, m in zip(scores, peaks)]
+                mixed = []
+                for on, e in zip(spots, powers):
+                    vp = qkv_in[w, :, 2 * width + on : 2 * width + on + pair]
+                    ones = jnp.ones_like(vp)
+                    low_out = jnp.dot(e[:cells], jnp.where(lanes, vp, ones), preferred_element_type=F32)
+                    high_out = jnp.dot(e[cells:], jnp.where(lanes, ones, vp), preferred_element_type=F32)
+                    total = pltpu.roll(jnp.where(lanes, high_out, low_out), head, 1)
+                    mixed.append((jnp.where(lanes, low_out, high_out) / total).astype(BF16))
+                att[w, 0:cells, spots[0] : spots[0] + 4 * pair] = jnp.concatenate(mixed, axis=1)
 
     def decode(at, x_in, outs):
         mixed = att[:, at, :].reshape(windows * half * WIN, width)
@@ -198,12 +205,6 @@
     wanted = (row_id % channels) * area + (row_id // channels) % PATCH * PATCH + row_id // (PATCH * channels)
     chosen = (col_id == wanted).astype(F32).astype(BF16)
     wdt[...] = lax.dot_general(chosen, wd[...], NT, preferred_element_type=F32).astype(BF16)
-
-    @pl.when(lat == n_lat - 1)
-    def _():
-        project(own.at[pl.ds(half, half)], edge.at[pl.ds(half, half)], xs_b, qkv_b, top_at)
-        attend(qkv_b, half * WIN, None)
-        decode(top_at, xs_b, [(is_high, d1), (is_low, send_side)])
 
     blocks = length // 16
 
@@ -259,17 +260,23 @@
         def _():
             top_copies[j].start()
 
+    decode(own_at, x_own, [(is_high, send_side), (is_low, d0)])
+
+    @pl.when(is_high)
+    def _():
+        to_low_now = remote(8, send_side, d1, lat, 0)
+        to_low_now.start()
+
+    @pl.when(lat == n_lat - 1)
+    def _():
+        project(own.at[pl.ds(half, half)], edge.at[pl.ds(half, half)], xs_b, qkv_b, top_at)
+        attend(qkv_b, half * WIN, None)
+        decode(top_at, xs_b, [(is_high, d1), (is_low, send_side)])
+
     @pl.when(side_high)
     def _():
         to_high_last = remote(7, send_side, d0, lat, 1)
         to_high_last.start()
-
-    decode(own_at, x_own, [(is_high, send_side), (is_low, d0)])
-
-    @pl.when(is_high)
-    def _():
-        to_low_now = remote(8, send_side, d1, lat, 0)
-        to_low_now.start()
 
     @pl.when(is_low)
     def _():

time: 78.9 us -> 70.9 us (0.90)
  Pallas kernels: 73.9 us -> 65.1 us
    pallas_call x1, Pallas kernels: 73.9 us -> 65.1 us  [body(): pl.pallas_call(functools.partial(cycle_kernel, sizes['lat']), out_shape=j...]
where the time goes in v3:
time: 70.9 us; the launch traced here: 70 us
  Pallas kernels  65.1 us (92%)
  local copies, waits for them, and re-layouts  4.8 us (7%)
    pallas_call x1, Pallas kernels, body(): pl.pallas_call(functools.partial(cycle_kernel, sizes['lat']), out_shape=j...  65.1 us
    transpose x1, local copies, waits for them, and re-layouts, body(): return advanced.transpose(1, 0, 2)  3.46 us

profile of v3, /device:TPU:27, one launch (start us, length us, event | category | flops | bytes accessed | tf_op | source)
XLA Modules:
  0.0 70.0 jit_solution(13959376551805734346)
XLA Ops:
  0.0 1.3 %copy.11.nudge_ref = f32[32,1]{1,0:T(8,128)} copy(f32[32,1]{0,1:T(1,128)} %bitcast.5) | data formatting | bytes 256 | tf_op jit(solution)/shard_map/broadcast_in_dim | solution.py:439
  1.3 65.1 %cycle.1 = f32[16,32,768]{2,1,0:T(8,128)} custom-call(bf16[8,96,1024]{2,1,0:T(8,128)(2,1)} %tokens.1, f32[32,32,384]{2,1,0:T(8,128)} %state.1, bf16[1024,1024]{1,0:T(8,128)(2,1)} %wq_hbm.1, bf16[1024,2048]{1,0:T(8,128)(2,1)} %wkv_hbm.1, bf16[1024,1024]{1,0:T(8,128)(2,1)} %wo_hbm.1, bf16[1024,512]{1,0:T(8,128)(2,1)} %wd_hbm.1, f32[1,1024]{1,0:T(1,128)} %bitcast.4, ...), custom_call_target="tpu_custom_call" | custom-call | tf_op jit(solution)/shard_map/cycle/pallas_call | solution.py:428
  66.5 3.5 %copy.12 = f32[32,16,768]{2,1,0:T(8,128)} copy(f32[32,16,768]{2,0,1:T(8,128)} %bitcast.3) | data formatting | bytes 3145728 | tf_op jit(solution)/shard_map/transpose | solution.py:442

commit v4 on v3

--- a/solution.py
+++ b/solution.py
@@ -3,6 +3,7 @@
 
 import jax
 import jax.numpy as jnp
+import ml_dtypes
 import numpy as np
 from jax import lax
 from jax.experimental import pallas as pl
@@ -24,12 +25,23 @@
 NT = (((1,), (1,)), ((), ()))
 
 
-def filter_rows(length, kept, stride):
+def filter_rows(length, kept, stride, first):
     offset = np.arange(length)
     waves = np.arange(1, kept)
     angles = 2.0 * np.pi * ((offset[:, None] * waves[None, :]) % length) / length
     kernel = (1.0 + 2.0 * np.cos(angles).sum(1)) / length
-    return kernel[(offset[None, :] - stride * np.arange(16)[:, None]) % length].astype(np.float32)
+    moved = offset[None, None, :] - stride * np.arange(16)[None, :, None] - np.asarray(first)[:, None, None]
+    rows = kernel[moved % length].astype(np.float32)
+    high = rows.astype(ml_dtypes.bfloat16)
+    return jnp.asarray(np.stack([high, (rows - high.astype(np.float32)).astype(ml_dtypes.bfloat16)]))
+
+
+def block_starts(length):
+    blocks = length // 16
+    per = blocks // PATCH
+    plain = [16 * g for g in range(blocks)]
+    patch = [((g % per * 16 + WIN // 2) * PATCH + g // per) % length for g in range(blocks)]
+    return plain, patch
 
 
 def split(value):
@@ -40,7 +52,7 @@
 def cycle_kernel(
     n_lat, tokens, state, wq_hbm, wkv_hbm, wo_hbm, wd_hbm, gain_ref, nudge_ref, rows1_ref, rows4_ref, out_ref,
     wqkv, wo, wd, wdt, own, recv, edge, corner, xs, xs_b, normed, qkv, qkv_b, att, lo,
-    band, base, high, low, dhigh, dlow, d0, d1, send_top, send_side, up_rows, down_rows, before, after, first,
+    band, base, high, low, dhigh, dlow, d0, d1, send_top, send_side, up_rows, down_rows, before, after, first, strength,
     load_sem, send_sem, recv_sem,
 ):
     lat, lon = lax.axis_index("lat"), lax.axis_index("lon")
@@ -143,7 +155,7 @@
         pair = 2 * head
         lanes = lax.broadcasted_iota(jnp.int32, (cells, pair), 1) < head
 
-        @pl.loop(0, windows)
+        @pl.loop(0, windows, unroll=2)
         def _(w):
             for group in range(0, HEADS // 2, 4):
                 spots = [p * pair for p in range(group, group + 4)]
@@ -206,15 +218,23 @@
     chosen = (col_id == wanted).astype(F32).astype(BF16)
     wdt[...] = lax.dot_general(chosen, wd[...], NT, preferred_element_type=F32).astype(BF16)
 
-    blocks = length // 16
-
-    @pl.loop(0, blocks)
-    def _(g):
-        on = pl.ds(pl.multiple_of(g * 16, 16), 16)
-        high[on, :], low[on, :] = split(pltpu.roll(rows1_ref[...], g * 16, 1))
-        per = blocks // PATCH
-        shift = lax.rem((lax.rem(g, per) * 16 + half) * PATCH + g // per, length)
-        dhigh[on, :], dlow[on, :] = split(pltpu.roll(rows4_ref[...], shift, 1))
+    @pl.when(lat == n_lat - 1)
+    def _():
+        project(own.at[pl.ds(half, half)], edge.at[pl.ds(half, half)], xs_b, qkv_b, top_at)
+
+    for starts, source, tables in zip(block_starts(length), (rows1_ref, rows4_ref), ((high, low), (dhigh, dlow))):
+        bases = sorted({start % 128 for start in starts})
+        for g, start in enumerate(starts):
+            cut = length - start // 128 * 128
+            for j in range(2):
+                value = source[j, bases.index(start % 128)]
+                if cut < length:
+                    value = jnp.concatenate([value[:, cut:], value[:, :cut]], axis=1)
+                tables[j][16 * g : 16 * g + 16, :] = value
+
+    eye = lax.broadcasted_iota(jnp.int32, (channels, channels), 0)
+    eye = eye == lax.broadcasted_iota(jnp.int32, (channels, channels), 1)
+    strength[...] = jnp.sum(jnp.where(eye, nudge_ref[...], 0.0), axis=1, keepdims=True)
 
     own_state.wait()
     state_copy.wait()
@@ -227,7 +247,7 @@
         kept = jnp.dot(s_high, high[...], preferred_element_type=F32)
         kept = kept + jnp.dot(s_low, high[...], preferred_element_type=F32)
         kept = kept + jnp.dot(s_high, low[...], preferred_element_type=F32)
-        kept = s.reshape(LEV, tall, length) - nudge_ref[on][:, :, None] * kept.reshape(LEV, tall, length)
+        kept = s.reshape(LEV, tall, length) - strength[on][:, :, None] * kept.reshape(LEV, tall, length)
         base[:, on, :] = jnp.swapaxes(kept, 0, 1)
 
     @pl.when(lat == 0)
@@ -269,7 +289,6 @@
 
     @pl.when(lat == n_lat - 1)
     def _():
-        project(own.at[pl.ds(half, half)], edge.at[pl.ds(half, half)], xs_b, qkv_b, top_at)
         attend(qkv_b, half * WIN, None)
         decode(top_at, xs_b, [(is_high, d1), (is_low, send_side)])
 
@@ -302,7 +321,7 @@
         kept = jnp.dot(x, dhigh[...], preferred_element_type=F32)
         kept = kept + jnp.dot(x, dlow[...], preferred_element_type=F32)
         y = r * PATCH
-        base[y : y + PATCH] = base[y : y + PATCH] + nudge_ref[...][None] * kept.reshape(PATCH, channels, length)
+        base[y : y + PATCH] = base[y : y + PATCH] + strength[...][None] * kept.reshape(PATCH, channels, length)
 
     up_lat, up_lon = jnp.where(is_low, lat, nxt), peer
     down_lat, down_lon = jnp.where(is_low, prev, lat), peer
@@ -422,8 +441,12 @@
         V(flow, BF16), V(flow, BF16), V(flow, BF16), V(flow, BF16),
         V((2, channels, length), BF16), V((2, channels, length), BF16),
         V((2, channels, length), BF16), V((2, channels, length), BF16),
-        V((tall + 2, channels, length), F32),
+        V((tall + 2, channels, length), F32), V((channels, 1), F32),
         pltpu.SemaphoreType.DMA((6,)), pltpu.SemaphoreType.DMA((11,)), pltpu.SemaphoreType.DMA((11,)),
+    ]
+    tables = [
+        filter_rows(length, KEEP, stride, sorted({start % 128 for start in starts}))
+        for stride, starts in zip((1, PATCH), block_starts(length))
     ]
     advanced = pl.pallas_call(
         functools.partial(cycle_kernel, sizes["lat"]),
@@ -436,8 +459,8 @@
         ),
         name="cycle",
     )(
-        tokens, state, w_query, w_keyval, w_out, w_dec, ln_gain[None], nudge[:, None],
-        jnp.asarray(filter_rows(length, KEEP, 1)), jnp.asarray(filter_rows(length, KEEP, PATCH)),
+        tokens, state, w_query, w_keyval, w_out, w_dec, ln_gain[None], nudge[None],
+        *tables,
     )
     return advanced.transpose(1, 0, 2)
 

time: 70.9 us -> 62 us (0.87)
  Pallas kernels: 65.1 us -> 57.7 us
  local copies, waits for them, and re-layouts: 4.8 us -> 3.46 us
    pallas_call x1, Pallas kernels: 65.1 us -> 57.7 us  [body(): pl.pallas_call(functools.partial(cycle_kernel, sizes['lat']), out_shape=j...]
    broadcast_in_dim x1 -> x0, local copies, waits for them, and re-layouts: 1.34 us -> none  [body(): nudge[:, None]]
where the time goes in v4:
time: 62 us; the launch traced here: 61.2 us
  Pallas kernels  57.7 us (93%)
  local copies, waits for them, and re-layouts  3.46 us (6%)
    pallas_call x1, Pallas kernels, body(): pl.pallas_call(functools.partial(cycle_kernel, sizes['lat']), out_shape=j...  57.7 us
    transpose x1, local copies, waits for them, and re-layouts, body(): return advanced.transpose(1, 0, 2)  3.46 us

profile of v4, /device:TPU:27, one launch (start us, length us, event | category | flops | bytes accessed | tf_op | source)
XLA Modules:
  0.0 61.2 jit_solution(11564326976184620696)
XLA Ops:
  0.0 57.7 %cycle.1 = f32[16,32,768]{2,1,0:T(8,128)} custom-call(bf16[8,96,1024]{2,1,0:T(8,128)(2,1)} %tokens.1, f32[32,32,384]{2,1,0:T(8,128)} %state.1, bf16[1024,1024]{1,0:T(8,128)(2,1)} %wq_hbm.1, bf16[1024,2048]{1,0:T(8,128)(2,1)} %wkv_hbm.1, bf16[1024,1024]{1,0:T(8,128)(2,1)} %wo_hbm.1, bf16[1024,512]{1,0:T(8,128)(2,1)} %wd_hbm.1, f32[1,1024]{1,0:T(1,128)} %bitcast.4, ...), custom_call_target="tpu_custom_call" | custom-call | tf_op jit(solution)/shard_map/cycle/pallas_call | solution.py:451
  57.7 3.5 %copy.11 = f32[32,16,768]{2,1,0:T(8,128)} copy(f32[32,16,768]{2,0,1:T(8,128)} %bitcast.3) | data formatting | bytes 3145728 | tf_op jit(solution)/shard_map/transpose | solution.py:465

commit v5 on v4

--- a/solution.py
+++ b/solution.py
@@ -384,7 +384,10 @@
     @pl.loop(0, tall)
     def _(y):
         second = tendency_row(first[y], first[y + 1], first[y + 2])
-        out_ref[y] = 0.5 * (base[y] + first[y + 1] + time_step * second)
+        base[y] = 0.5 * (base[y] + first[y + 1] + time_step * second)
+
+    for g in range(0, tall, 8):
+        out_ref[:, g : g + 8, :] = jnp.swapaxes(base[g : g + 8], 0, 1)
 
     @pl.when(has_next)
     def _():
@@ -450,7 +453,7 @@
     ]
     advanced = pl.pallas_call(
         functools.partial(cycle_kernel, sizes["lat"]),
-        out_shape=jax.ShapeDtypeStruct(field, F32),
+        out_shape=jax.ShapeDtypeStruct((channels, tall, length), F32),
         in_specs=[hbm] * 6 + [vmem] * 4,
         out_specs=vmem,
         scratch_shapes=scratch,
@@ -462,7 +465,7 @@
         tokens, state, w_query, w_keyval, w_out, w_dec, ln_gain[None], nudge[None],
         *tables,
     )
-    return advanced.transpose(1, 0, 2)
+    return advanced
 
 
 def tendency_row(south, centre, north):

time: 62 us -> 61.5 us (level)
  local copies, waits for them, and re-layouts: 3.46 us -> 2.66 us
    transpose x1 -> x0, local copies, waits for them, and re-layouts: 3.46 us -> none  [body(): return advanced.transpose(1, 0, 2)]
    unnamed x0 -> x1, local copies, waits for them, and re-layouts: none -> 2.66 us
where the time goes in v5:
time: 61.5 us; the launch traced here: 60.7 us
  Pallas kernels  58 us (94%)
  local copies, waits for them, and re-layouts  2.66 us (4%)
    pallas_call x1, Pallas kernels, body(): pl.pallas_call(functools.partial(cycle_kernel, sizes['lat']), out_shape=j...  58 us
    unnamed x1, local copies, waits for them, and re-layouts  2.66 us

profile of v5, /device:TPU:27, one launch (start us, length us, event | category | flops | bytes accessed | tf_op | source)
XLA Modules:
  0.0 60.7 jit_solution(1719349207832772165)
XLA Ops:
  0.0 58.0 %cycle.1 = f32[32,16,768]{2,1,0:T(8,128)} custom-call(bf16[8,96,1024]{2,1,0:T(8,128)(2,1)} %tokens.1, f32[32,32,384]{2,1,0:T(8,128)} %state.1, bf16[1024,1024]{1,0:T(8,128)(2,1)} %wq_hbm.1, bf16[1024,2048]{1,0:T(8,128)(2,1)} %wkv_hbm.1, bf16[1024,1024]{1,0:T(8,128)(2,1)} %wo_hbm.1, bf16[1024,512]{1,0:T(8,128)(2,1)} %wd_hbm.1, f32[1,1024]{1,0:T(1,128)} %bitcast.2, ...), custom_call_target="tpu_custom_call" | custom-call | tf_op jit(solution)/shard_map/cycle/pallas_call | solution.py:454
  58.0 2.7 %copy.12 = f32[32,16,768]{2,1,0:T(8,128)} copy(f32[32,16,768]{2,1,0:T(8,128)} %cycle.1) | data formatting | bytes 3145728
